TPU v7x, 256 devices: a whole 4x4x8 slice. The times are simulated.
256 devices in a mesh: wide: 32 (over x, z), narrow: 8 (over y, core).
Axes of the slice: x: 4, y: 4, z: 8, core: 2. Of those that a mesh axis runs over, the one named last changes fastest.
Arguments:
- pdfs: float32 [19, 1024, 8192], P(None, 'wide', 'narrow'), may hold values from 0.05 to 1
- link_flags: int32 [2, 1024, 8192], P(None, 'wide', 'narrow'), may hold values from 0 to 1022, as said below
- block_level: int32 [32, 8], P('wide', 'narrow'), may hold values from 0 to 1
- grain_pos: float32 [3, 262144], P(None, ('wide', 'narrow')), may hold values from 0 to 32
- grain_vel: float32 [3, 262144], P(None, ('wide', 'narrow')), may hold values from -3 to 3
- grain_radius: float32 [262144], P(('wide', 'narrow')), may hold values from 0.5 to 1.5
- grain_cell: int32 [262144], P(('wide', 'narrow')), may hold values from 0 to 32767
- contact_pairs: int32 [2, 786432], P(None, ('wide', 'narrow')), may hold values from 0 to 1023
- contact_spring: float32 [3, 786432], P(None, ('wide', 'narrow')), may hold values from -6 to 6
- iface_source: int32 [262144], P(('wide', 'narrow')), may hold values from 0 to 32767
- iface_offset: int32 [1024], replicated, may hold values from -2 to 2, as said below
- iface_slot: int32 [1024], replicated, may hold values from 0 to 1023, each once
- iface_target: int32 [262144], P(('wide', 'narrow')), may hold values from 0 to 32767, as said below
- migrant_slots: int32 [2, 16384], P(None, ('wide', 'narrow')), may hold values from 0 to 1023, as said below
Outputs:
- pdfs_next: float32 [19, 1024, 8192], P(None, 'wide', 'narrow')
- grain_pos_next: float32 [3, 262144], P(None, ('wide', 'narrow'))
- grain_vel_next: float32 [3, 262144], P(None, ('wide', 'narrow'))
- grain_radius_next: float32 [262144], P(('wide', 'narrow'))
- contact_spring_next: float32 [3, 786432], P(None, ('wide', 'narrow'))
Inputs may be any that keep to these rules, and one draw needn't show every extreme that they name: `iface_offset`: each of -2, -1, 0, 1, 2 occurs; each nonzero value occurs at most 1024 // 4 times, and one of them exactly so; the same row r goes the same number of blocks along the length from every block, staying at its place across the width. `iface_slot`: the same for every block. `iface_target`: distinct within a block. `iface_source`: local cell indices. `migrant_slots`: the 128 slots of a block are distinct; every block sends exactly 64 grains each way. `contact_pairs`: slots of grains of the same block. `grain_cell`: local cell indices. `link_flags`: bit 0 of row 0 is never set and row 1 uses bits 0 to 8 only; in the bottom layer (z = 0) the links of all directions with c_z = 1 are solid, in the top layer those with c_z = -1.
All inputs are finite; a program needn't handle non-finite values.
Results may differ from a plain program's by a relative error of at most 0.00002.
Values sent between devices are 32-bit elements; how exact they have to be, the bound alone decides.
A program may use at most 128 MiB of HBM per device.

v0:
```python
import functools

import jax
import jax.numpy as jnp
from jax import lax
from jax.experimental import pallas as pl
from jax.experimental.pallas import tpu as pltpu
from jax.sharding import PartitionSpec as P

VELOCITY = (
    (0, 0, 0), (1, 0, 0), (-1, 0, 0), (0, 1, 0), (0, -1, 0), (0, 0, 1), (0, 0, -1),
    (1, 1, 0), (-1, -1, 0), (1, -1, 0), (-1, 1, 0), (1, 0, 1), (-1, 0, -1), (1, 0, -1),
    (-1, 0, 1), (0, 1, 1), (0, -1, -1), (0, 1, -1), (0, -1, 1),
)
OPPOSITE = (0, 2, 1, 4, 3, 6, 5, 8, 7, 10, 9, 12, 11, 14, 13, 16, 15, 18, 17)
tau_coarse = 1.0
tau_fine = 1.5
drag_coef = 0.5
mass_coef = 10.0
spring_coef = 0.2
dashpot_coef = 0.05
gravity_z = -0.01
blend_coef = 0.5

NX = 32
NYZ = 1024
TOP = 8
EXT = NX + 16
X_PLUS = (1, 7, 9, 11, 13)
X_MINUS = (2, 8, 10, 12, 14)
Y_PLUS = (3, 7, 10, 15, 17)
Y_MINUS = (4, 8, 9, 16, 18)
DISTANCE = (-2, 2, -1, 1)
MESH = pl.DeviceIdType.MESH
F32 = jnp.float32
BF16 = jnp.bfloat16
NT = (((1,), (1,)), ((), ()))
NN = (((1,), (0,)), ((), ()))


def iota(shape, axis):
    return lax.broadcasted_iota(jnp.int32, shape, axis)


def split2(value):
    high = value.astype(BF16).astype(F32)
    return high, value - high


def split3(value):
    high = value.astype(BF16).astype(F32)
    rest = value - high
    middle = rest.astype(BF16).astype(F32)
    return high, middle, rest - middle


def one_hot(row, size, start=0):
    lanes = row.shape[1]
    return jnp.where(iota((size, lanes), 0) + start == row, 1.0, 0.0).astype(BF16)


def fill_one_hot(ref, row):
    step = 128

    @pl.loop(0, NYZ // step)
    def _(i):
        start = pl.multiple_of(i * step, step)
        ref[pl.ds(start, step), :] = one_hot(row, step, start)


def dot(a, b, dims):
    return lax.dot_general(a, b, dims, preferred_element_type=F32)


def pack_interface(off_ref, slot_ref, src_ref, tgt_ref):
    off = off_ref[...]
    s8 = iota((8, NYZ), 0)
    dval = jnp.where(s8 == 0, DISTANCE[0], jnp.where(s8 == 1, DISTANCE[1], jnp.where(s8 == 2, DISTANCE[2], jnp.where(
        s8 == 3, DISTANCE[3], jnp.where(s8 == 4, 0, 99)))))
    member = jnp.where(off == dval, 1.0, 0.0)
    blocks = [member[:, b * 128:(b + 1) * 128] for b in range(8)]
    before = jnp.where(iota((128, 128), 0) < iota((128, 128), 1), 1.0, 0.0).astype(BF16)
    local = dot(jnp.concatenate(blocks, axis=0).astype(BF16), before, NN)
    running = jnp.zeros((8, 1), F32)
    ranks = []
    for b in range(8):
        ranks.append(local[b * 8:(b + 1) * 8] + running)
        running = running + jnp.sum(blocks[b], axis=1, keepdims=True)
    counts = [running[i:i + 1, :] for i in range(4)]
    ends = []
    total = jnp.zeros((1, 1), F32)
    for i in range(4):
        total = total + (256.0 - counts[i])
        ends.append(total)
    s128 = iota((8, 128), 0)
    base = (s128 * 256).astype(F32)
    positions = []
    for b in range(8):
        sent = jnp.sum(jnp.where(s128 < 4, blocks[b] * (base + ranks[b]), 0.0), axis=0, keepdims=True)
        z = ranks[b][4:5]
        stay = 768.0 + counts[3] + z - ends[2]
        for i in (2, 1, 0):
            start = ends[i - 1] if i else 0.0
            stay = jnp.where(z < ends[i], 256.0 * i + counts[i] + z - start, stay)
        positions.append(sent + blocks[b][4:5] * stay)
    pos = jnp.concatenate(positions, axis=1).astype(jnp.int32)
    src = src_ref[...]
    slot = slot_ref[...]
    values = jnp.where(s8 == 0, src >> 8, jnp.where(s8 == 1, src & 255, jnp.where(s8 == 2, slot >> 8, jnp.where(
        s8 == 3, slot & 255, 0)))).astype(F32)
    pos_high = pos >> 7
    stacked = jnp.concatenate([jnp.where(pos_high == h, values, 0.0) for h in range(8)], axis=0).astype(BF16)
    packed = dot(stacked, one_hot(pos & 127, 128), NT)
    src_packed = jnp.concatenate([packed[h * 8:h * 8 + 1] * 256.0 + packed[h * 8 + 1:h * 8 + 2] for h in range(8)], axis=1)
    slot_high = jnp.concatenate([packed[h * 8 + 2:h * 8 + 3] for h in range(8)], axis=1).astype(jnp.int32)
    slot_low = jnp.concatenate([packed[h * 8 + 3:h * 8 + 4] for h in range(8)], axis=1).astype(jnp.int32)
    slot_packed = slot_high * 256 + slot_low
    tgt = tgt_ref[...]
    table = jnp.concatenate([(tgt >> 8).astype(F32), (tgt & 255).astype(F32)], axis=0).astype(BF16)
    found = dot(table, one_hot(slot_packed & 127, 128), NN)
    chosen = s8 == (slot_packed >> 7)
    tgt_high = jnp.sum(jnp.where(chosen, found[0:8], 0.0), axis=0, keepdims=True)
    tgt_low = jnp.sum(jnp.where(chosen, found[8:16], 0.0), axis=0, keepdims=True)
    tgt_packed = (tgt_high * 256.0 + tgt_low).astype(jnp.int32)
    return src_packed.astype(jnp.int32), tgt_packed, counts


def step_kernel(
    pdfs_hbm, flags_hbm, level_ref, pos_ref, vel_ref, rad_ref, cell_ref, pairs_ref, spring_ref, src_ref, off_ref, slot_ref,
    tgt_ref, mig_ref,
    read_ref, arrived_ref, tgtp_ref, state_ref, newcomers_ref, spring_out_ref,
    pdfs, flags, onehot, moved_in, ext, velf, velb, rows16, edge_x, edge_y, edge_c, halo_x, halo_y, halo_yp, halo_c, splits, gathered,
    received, leaving, joined, fluid, force,
    load_sem, send_sem, recv_sem,
):
    a, b = lax.axis_index("wide"), lax.axis_index("narrow")
    n_wide, n_narrow = lax.axis_size("wide"), lax.axis_size("narrow")

    def device(dx, dy):
        return (lax.rem(a + dx + n_wide, n_wide), lax.rem(b + dy + n_narrow, n_narrow))

    load_p = pltpu.make_async_copy(pdfs_hbm, pdfs, load_sem.at[0])
    load_f = pltpu.make_async_copy(flags_hbm, flags, load_sem.at[1])
    load_p.start()
    load_f.start()
    around = [(dx, dy) for dx in (-1, 0, 1) for dy in (-1, 0, 1) if dx or dy] + [(-2, 0), (2, 0)]
    barrier = pltpu.get_barrier_semaphore()
    for dx, dy in around:
        pl.semaphore_signal(barrier, inc=1, device_id=device(dx, dy), device_id_type=MESH)

    cell = cell_ref[...]
    grain_x = cell >> 10
    fill_one_hot(onehot, cell & 1023)
    drag = drag_coef * rad_ref[...]
    in_row = iota((NX, NYZ), 0) == grain_x
    weights = [drag] + [drag * vel_ref[c:c + 1, :] for c in range(3)]
    for k, weight in enumerate(weights):
        for part, value in enumerate(split2(weight)):
            moved_in[pl.ds((part * 4 + k) * NX, NX), :] = jnp.where(in_row, value, 0.0).astype(BF16)

    @pl.loop(0, 4)
    def _(i):
        cols = pl.ds(pl.multiple_of(i * 256, 256), 256)
        got = dot(moved_in[...], onehot[cols, :], NT)
        force[:, cols] = got[0:128] + got[128:256]

    level = level_ref[0, 0]
    tau = jnp.where(level == 1, tau_fine, tau_coarse).astype(F32)
    omega = jnp.where(level == 1, 1.0 / tau_fine, 1.0 / tau_coarse).astype(F32)
    keep = jnp.where(level == 1, 1.0 - 1.0 / tau_fine, 0.0).astype(F32)
    load_p.wait()

    @pl.loop(0, 32)
    def _(i):
        row = pl.multiple_of((i // 8) * 8, 8)
        rows = pl.ds(row, 8)
        cols = pl.ds(pl.multiple_of((i % 8) * 128, 128), 128)
        p = [pdfs[q, rows, cols] for q in range(19)]
        pair_sum = {q: p[q] + p[q + 1] for q in range(1, 19, 2)}
        pair_dif = {q: p[q] - p[q + 1] for q in range(1, 19, 2)}
        density = p[0] + ((pair_sum[1] + pair_sum[3]) + (pair_sum[5] + pair_sum[7])) + (
            (pair_sum[9] + pair_sum[11]) + (pair_sum[13] + pair_sum[15]) + pair_sum[17])
        mom = (
            (pair_dif[1] + pair_dif[7]) + (pair_dif[9] + pair_dif[11]) + pair_dif[13],
            (pair_dif[3] + pair_dif[7]) + (pair_dif[15] - pair_dif[9]) + pair_dif[17],
            (pair_dif[5] + pair_dif[11]) + (pair_dif[15] - pair_dif[13]) - pair_dif[17],
        )
        inverse = 1.0 / density
        pull = tau * inverse
        resist = force[pl.ds(row, 8), cols]
        shifted = []
        for c in range(3):
            v = mom[c] * inverse
            velf[pl.ds(c * NX + row, 8), cols] = v
            shifted.append(v + pull * (force[pl.ds((c + 1) * NX + row, 8), cols] - v * resist))
        square = 1.5 * (shifted[0] * shifted[0] + shifted[1] * shifted[1] + shifted[2] * shifted[2])
        base = 1.0 - square
        dense = omega * density
        out_rows = pl.ds(TOP + row, 8)
        ext[0, out_rows, cols] = keep * p[0] + (dense * (1.0 / 3.0)) * base
        for q in range(1, 19, 2):
            along = None
            for c in range(3):
                if VELOCITY[q][c] == 1:
                    along = shifted[c] if along is None else along + shifted[c]
                elif VELOCITY[q][c] == -1:
                    along = along - shifted[c]
            scaled = dense * (1.0 / 18.0 if q < 7 else 1.0 / 36.0)
            even = scaled * (base + 4.5 * along * along)
            odd = scaled * (3.0 * along)
            ext[q, out_rows, cols] = keep * p[q] + (even + odd)
            ext[q + 1, out_rows, cols] = keep * p[q + 1] + (even - odd)

    for k in range(5):
        edge_x[0, k:k + 1, :] = ext[X_PLUS[k], TOP + NX - 1:TOP + NX, :]
        edge_x[1, k:k + 1, :] = ext[X_MINUS[k], TOP:TOP + 1, :]
        edge_y[0, k] = ext[Y_PLUS[k], TOP:TOP + NX, 896:1024]
        edge_y[1, k] = ext[Y_MINUS[k], TOP:TOP + NX, 0:128]
    edge_c[0, 0:1, :] = ext[7, TOP + NX - 1:TOP + NX, 896:1024]
    edge_c[1, 0:1, :] = ext[8, TOP:TOP + 1, 0:128]
    edge_c[2, 0:1, :] = ext[9, TOP + NX - 1:TOP + NX, 0:128]
    edge_c[3, 0:1, :] = ext[10, TOP:TOP + 1, 896:1024]
    pl.semaphore_wait(barrier, len(around))

    def send(index, source, target, dx, dy):
        copy = pltpu.make_async_remote_copy(
            src_ref=source, dst_ref=target, send_sem=send_sem.at[index], recv_sem=recv_sem.at[index],
            device_id=device(dx, dy), device_id_type=MESH)
        copy.start()
        return copy

    halo = [
        send(0, edge_x.at[0], halo_x.at[0], 1, 0),
        send(1, edge_x.at[1], halo_x.at[1], -1, 0),
        send(2, edge_y.at[0], halo_y.at[0], 0, 1),
        send(3, edge_y.at[1], halo_y.at[1], 0, -1),
        send(4, edge_c.at[0], halo_c.at[0], 1, 1),
        send(5, edge_c.at[1], halo_c.at[1], -1, -1),
        send(6, edge_c.at[2], halo_c.at[2], 1, -1),
        send(7, edge_c.at[3], halo_c.at[3], -1, 1),
    ]

    for part, value in enumerate(split2(velf[...])):
        velb[pl.ds(part * 96, 96), :] = value.astype(BF16)

    @pl.loop(0, 4)
    def _(i):
        cols = pl.ds(pl.multiple_of(i * 256, 256), 256)
        got = dot(velb[...], onehot[:, cols], NN)
        got = got[0:96] + got[96:192]
        here = iota((NX, 256), 0) == (cell_ref[:, cols] >> 10)
        for c in range(3):
            fluid[c:c + 1, cols] = jnp.sum(jnp.where(here, got[c * NX:(c + 1) * NX], 0.0), axis=0, keepdims=True)

    pair_index = jnp.concatenate([pairs_ref[0:1, :], pairs_ref[1:2, :]], axis=1)
    pair_high = pair_index >> 7
    pair_hot = one_hot(pair_index & 127, 128)
    vel = vel_ref[...]
    rows16[...] = jnp.zeros_like(rows16)
    for part, value in enumerate(split3(vel)):
        rows16[part * 3:part * 3 + 3, 0:NYZ] = value
    table = jnp.concatenate([rows16[:, h * 128:(h + 1) * 128] for h in range(8)], axis=0).astype(BF16)
    found = dot(table, pair_hot, NN)
    at_pair = jnp.where(pair_high == 0, found[0:16], 0.0)
    for h in range(1, 8):
        at_pair = jnp.where(pair_high == h, found[h * 16:(h + 1) * 16], at_pair)
    at_pair = at_pair[0:3] + at_pair[3:6] + at_pair[6:9]
    relative = at_pair[:, 3072:6144] - at_pair[:, 0:3072]
    spring = spring_ref[...]
    spring_out_ref[...] = spring + relative
    contact = spring_coef * spring + dashpot_coef * relative
    for part, value in enumerate(split3(contact)):
        rows16[part * 3:part * 3 + 3, 0:3072] = value
        rows16[part * 3:part * 3 + 3, 3072:6144] = -value
    both = rows16[...]
    spread = jnp.concatenate([jnp.where(pair_high == h, both, 0.0).astype(BF16) for h in range(8)], axis=0)
    summed = dot(spread, pair_hot, NT)
    parts = [summed[h * 16:h * 16 + 3] + summed[h * 16 + 3:h * 16 + 6] + summed[h * 16 + 6:h * 16 + 9] for h in range(8)]
    summed = jnp.concatenate(parts, axis=1)
    radius = rad_ref[...]
    total = (drag_coef * radius) * (fluid[0:3, :] - vel) + summed
    mass = mass_coef * radius * radius * radius
    falling = jnp.where(iota((3, NYZ), 0) == 2, gravity_z, 0.0)
    moved_vel = vel + total / mass + falling
    state_ref[0:3, :] = pos_ref[...] + moved_vel
    state_ref[3:6, :] = moved_vel
    state_ref[6:7, :] = radius
    state_ref[7:8, :] = jnp.ones_like(radius)

    slots = jnp.concatenate([mig_ref[0:1, :], mig_ref[1:2, :]], axis=1)
    mig_hot = one_hot(slots, NYZ)
    state = jnp.concatenate(split3(state_ref[...]), axis=0).astype(BF16)
    out = dot(state, mig_hot, NN)
    leaving[...] = out[0:8] + out[8:16] + out[16:24]
    migrate = [send(8, leaving, joined.at[0], -1, 0), send(9, leaving, joined.at[1], 1, 0)]

    src_packed, tgt_packed, counts = pack_interface(off_ref, slot_ref, src_ref, tgt_ref)
    tgtp_ref[...] = tgt_packed
    fill_one_hot(onehot, src_packed & 1023)

    load_f.wait()
    for copy in halo:
        copy.wait()
    for k in range(5):
        ext[X_PLUS[k], TOP - 1:TOP, :] = halo_x[0, k:k + 1, :]
        ext[X_MINUS[k], TOP + NX:TOP + NX + 1, :] = halo_x[1, k:k + 1, :]
        for side in range(2):
            halo_yp[side, k, TOP:TOP + NX, :] = halo_y[side, k]
    halo_yp[0, 1, TOP - 1:TOP, :] = halo_c[0, 0:1, :]
    halo_yp[1, 1, TOP + NX:TOP + NX + 1, :] = halo_c[1, 0:1, :]
    halo_yp[1, 2, TOP - 1:TOP, :] = halo_c[2, 0:1, :]
    halo_yp[0, 2, TOP + NX:TOP + NX + 1, :] = halo_c[3, 0:1, :]
    lane = iota((NX, 128), 1)
    for q in range(19):
        cx, cy, cz = VELOCITY[q]
        shift = cy * 32 + cz
        rows = slice(TOP - cx, TOP - cx + NX)
        value = ext[q, rows, :]
        if shift:
            value = pltpu.roll(value, shift % NYZ, 1)
        if cy == 1:
            edge = pltpu.roll(halo_yp[0, Y_PLUS.index(q), rows, :], shift % 128, 1)
            value = jnp.concatenate([jnp.where(lane < 32, edge, value[:, 0:128]), value[:, 128:]], axis=1)
        if cy == -1:
            edge = halo_yp[1, Y_MINUS.index(q), rows, :]
            edge = pltpu.roll(edge, shift % 128, 1)
            value = jnp.concatenate([value[:, :896], jnp.where(lane >= 96, edge, value[:, 896:])], axis=1)
        if q:
            bit = 1 << (q if q < 10 else q - 10)
            solid = (flags[0 if q < 10 else 1] & bit) != 0
            value = jnp.where(solid, ext[OPPOSITE[q], TOP:TOP + NX, :], value)
        read_ref[q] = value
        high, low = split2(value)
        splits[pl.ds(q * NX, NX), :] = high.astype(BF16)
        splits[pl.ds((19 + q) * NX, NX), :] = low.astype(BF16)

    rows_out = []
    for i in range(4):
        cols = slice(i * 256, (i + 1) * 256)
        got = dot(splits[...], onehot[:, cols], NN)
        here = iota((NX, 256), 0) == (src_packed[:, cols] >> 10)
        for q in range(19):
            both_parts = got[q * NX:(q + 1) * NX] + got[(19 + q) * NX:(20 + q) * NX]
            gathered[i, q:q + 1, :] = jnp.sum(jnp.where(here, both_parts, 0.0), axis=0, keepdims=True)
        rows_out.append(send(10 + i, gathered.at[i], received.at[i], DISTANCE[i], 0))

    for copy in migrate:
        copy.wait()
    mig_lane = iota((8, 128), 1)
    change = jnp.where(iota((8, 128), 0) == 0, jnp.where(mig_lane < 64, float(NX), -float(NX)), 0.0)
    newcomers_ref[...] = jnp.where(mig_lane < 64, joined[0], joined[1]) + change
    for i in range(4):
        rows_out[i].wait()
        stays = iota((24, 256), 1).astype(F32) >= counts[i]
        arrived_ref[:, i * 256:(i + 1) * 256] = jnp.where(stays, gathered[i], received[i])


def finish_kernel(
    read_ref, arrived_ref, tgtp_ref, state_ref, newcomers_ref, mig_ref, spring_ref,
    next_ref, pos_ref, vel_ref, rad_ref, spring_out_ref,
    spread,
):
    step = pl.program_id(0)
    target = tgtp_ref[...]

    @pl.when(step == 0)
    def _():
        here = iota((NX, NYZ), 0) == (target >> 10)
        for q in range(19):
            for part, value in enumerate(split2(arrived_ref[q:q + 1, :])):
                spread[pl.ds((part * 19 + q) * NX, NX), :] = jnp.where(here, value, 0.0).astype(BF16)
        spread[pl.ds(38 * NX, NX), :] = jnp.where(here, 1.0, 0.0).astype(BF16)
        slots = jnp.concatenate([mig_ref[0:1, :], mig_ref[1:2, :]], axis=1)
        mig_hot = one_hot(slots, NYZ)
        arrived = jnp.concatenate(split3(newcomers_ref[...]), axis=0).astype(BF16)
        placed = dot(arrived, mig_hot, NT)
        placed = placed[0:8] + placed[8:16] + placed[16:24]
        result = jnp.where(placed[7:8] > 0.5, placed, state_ref[...])
        pos_ref[...] = result[0:3]
        vel_ref[...] = result[3:6]
        rad_ref[...] = result[6:7]
        spring_out_ref[...] = spring_ref[...]

    hot = one_hot(target & 1023, 256, step * 256)
    got = dot(spread[...], hot, NT)
    hit = got[38 * NX:39 * NX] > 0.5
    for q in range(19):
        value = read_ref[q]
        carried = got[q * NX:(q + 1) * NX] + got[(19 + q) * NX:(20 + q) * NX]
        next_ref[q] = jnp.where(hit, blend_coef * (value + carried), value)


def shards(
    pdfs, link_flags, block_level, grain_pos, grain_vel, grain_radius, grain_cell, contact_pairs, contact_spring, iface_source,
    iface_offset, iface_slot, iface_target, migrant_slots,
):
    row = (1, NYZ)
    vmem = pl.BlockSpec(memory_space=pltpu.VMEM)
    hbm = pl.BlockSpec(memory_space=pl.ANY)
    outs = pl.pallas_call(
        step_kernel,
        name="step",
        out_shape=(
            jax.ShapeDtypeStruct((19, NX, NYZ), F32),
            jax.ShapeDtypeStruct((24, NYZ), F32),
            jax.ShapeDtypeStruct(row, jnp.int32),
            jax.ShapeDtypeStruct((8, NYZ), F32),
            jax.ShapeDtypeStruct((8, 128), F32),
            jax.ShapeDtypeStruct((3, 3072), F32),
        ),
        in_specs=[hbm, hbm, pl.BlockSpec(memory_space=pltpu.SMEM)] + [vmem] * 11,
        out_specs=(vmem,) * 6,
        scratch_shapes=[
            pltpu.VMEM((19, NX, NYZ), F32),
            pltpu.VMEM((2, NX, NYZ), jnp.int32),
            pltpu.VMEM((NYZ, NYZ), BF16),
            pltpu.VMEM((8 * NX, NYZ), BF16),
            pltpu.VMEM((19, EXT, NYZ), F32),
            pltpu.VMEM((3 * NX, NYZ), F32),
            pltpu.VMEM((6 * NX, NYZ), BF16),
            pltpu.VMEM((16, 6144), F32),
            pltpu.VMEM((2, 8, NYZ), F32),
            pltpu.VMEM((2, 5, NX, 128), F32),
            pltpu.VMEM((4, 8, 128), F32),
            pltpu.VMEM((2, 8, NYZ), F32),
            pltpu.VMEM((2, 5, NX, 128), F32),
            pltpu.VMEM((2, 5, EXT, 128), F32),
            pltpu.VMEM((4, 8, 128), F32),
            pltpu.VMEM((38 * NX, NYZ), BF16),
            pltpu.VMEM((4, 24, 256), F32),
            pltpu.VMEM((4, 24, 256), F32),
            pltpu.VMEM((8, 128), F32),
            pltpu.VMEM((2, 8, 128), F32),
            pltpu.VMEM((8, NYZ), F32),
            pltpu.VMEM((4 * NX, NYZ), F32),
            pltpu.SemaphoreType.DMA((2,)),
            pltpu.SemaphoreType.DMA((14,)),
            pltpu.SemaphoreType.DMA((14,)),
        ],
        compiler_params=pltpu.CompilerParams(collective_id=0, has_side_effects=True, vmem_limit_bytes=56 << 20),
    )(
        pdfs, link_flags, block_level, grain_pos, grain_vel, grain_radius.reshape(row), grain_cell.reshape(row), contact_pairs,
        contact_spring, iface_source.reshape(row), iface_offset.reshape(row), iface_slot.reshape(row),
        iface_target.reshape(8, 128), migrant_slots,
    )
    read, arrived, tgtp, state, newcomers, spring_next = outs

    def whole(shape):
        return pl.BlockSpec(shape, lambda i: (0,) * len(shape))

    block = pl.BlockSpec((19, NX, 256), lambda i: (0, 0, i))
    result = pl.pallas_call(
        finish_kernel,
        name="finish",
        grid=(4,),
        out_shape=(
            jax.ShapeDtypeStruct((19, NX, NYZ), F32),
            jax.ShapeDtypeStruct((3, NYZ), F32),
            jax.ShapeDtypeStruct((3, NYZ), F32),
            jax.ShapeDtypeStruct(row, F32),
            jax.ShapeDtypeStruct((3, 3072), F32),
        ),
        in_specs=[block, whole((24, NYZ)), whole(row), whole((8, NYZ)), whole((8, 128)), whole((2, 64)), whole((3, 3072))],
        out_specs=(block, whole((3, NYZ)), whole((3, NYZ)), whole(row), whole((3, 3072))),
        scratch_shapes=[pltpu.VMEM((39 * NX, NYZ), BF16)],
        compiler_params=pltpu.CompilerParams(dimension_semantics=("arbitrary",), vmem_limit_bytes=40 << 20),
    )(read, arrived, tgtp, state, newcomers, migrant_slots, spring_next)
    pdfs_next, pos_next, vel_next, rad_next, spring_out = result
    return pdfs_next, pos_next, vel_next, rad_next.reshape(NYZ), spring_out


def solution(mesh):
    both = ("wide", "narrow")
    in_specs = (
        P(None, "wide", "narrow"), P(None, "wide", "narrow"), P("wide", "narrow"), P(None, both), P(None, both), P(both), P(both),
        P(None, both), P(None, both), P(both), P(), P(), P(both), P(None, both),
    )
    out_specs = (P(None, "wide", "narrow"), P(None, both), P(None, both), P(both), P(None, both))
    return jax.shard_map(shards, mesh=mesh, in_specs=in_specs, out_specs=out_specs, check_vma=False)
```

profile of v0, /device:TPU:1, one launch (start us, length us, event | category | flops | bytes accessed | tf_op | source)
XLA Modules:
  0.0 40.2 jit_solution(10288328379716325221)
XLA Ops:
  0.6 0.0 copy-start.4
  1.3 27.8 %step.1 = (f32[19,32,1024]{2,1,0:T(8,128)}, f32[24,1024]{1,0:T(8,128)}, s32[1,1024]{1,0:T(1,128)}, f32[8,1024]{1,0:T(8,128)}, f32[8,128]{1,0:T(8,128)}, /*index=5*/f32[3,3072]{1,0:T(4,128)}) custom-call(f32[19,32,1024]{2,1,0:T(8,128)} %pdfs_hbm.1, s32[2,32,1024]{2,1,0:T(8,128)} %flags_hbm.1, s32[1,1]{1,0:T(1,128)S(6)} %copy.19.level_ref, f32[3,1024]{1,0:T(4,128)} %pos_ref.1, ...), custom_call_target="tpu_custom_call" | custom-call | tf_op jit(solution)/shard_map/step/pallas_call | solution.py:400
  29.1 0.0 copy-done.4
  29.1 0.0 copy-start
  29.1 1.7 %copy-done = f32[19,32,1024]{2,1,0:T(8,128)S(1)} copy-done((f32[19,32,1024]{2,1,0:T(8,128)S(1)}, f32[19,32,1024]{2,1,0:T(8,128)}, u32[]{:S(2)}) %copy-start) | copy-done | bytes 2490392
  30.8 0.0 copy-start.1
  30.8 0.9 %copy-done.1 = f32[24,1024]{1,0:T(8,128)S(1)} copy-done((f32[24,1024]{1,0:T(8,128)S(1)}, f32[24,1024]{1,0:T(8,128)}, u32[]{:S(2)}) %copy-start.1) | copy-done | bytes 98328
  31.7 0.0 copy-start.2
  31.7 0.8 %copy-done.2 = f32[3,3072]{1,0:T(4,128)S(1)} copy-done((f32[3,3072]{1,0:T(4,128)S(1)}, f32[3,3072]{1,0:T(4,128)}, u32[]{:S(2)}) %copy-start.2) | copy-done | bytes 36888
  32.5 0.0 copy-start.3
  32.5 0.8 %copy-done.3 = f32[8,1024]{1,0:T(8,128)S(1)} copy-done((f32[8,1024]{1,0:T(8,128)S(1)}, f32[8,1024]{1,0:T(8,128)}, u32[]{:S(2)}) %copy-start.3) | copy-done | bytes 32792
  33.3 0.0 copy-start.5
  33.3 0.7 %copy-done.5 = s32[1,1024]{1,0:T(1,128)S(1)} copy-done((s32[1,1024]{1,0:T(1,128)S(1)}, s32[1,1024]{1,0:T(1,128)}, u32[]{:S(2)}) %copy-start.5) | copy-done | bytes 4120
  33.9 0.0 copy-start.6
  33.9 0.7 %copy-done.6 = f32[8,128]{1,0:T(8,128)S(1)} copy-done((f32[8,128]{1,0:T(8,128)S(1)}, f32[8,128]{1,0:T(8,128)}, u32[]{:S(2)}) %copy-start.6) | copy-done | bytes 4120
  34.6 5.5 %finish.1 = (f32[19,32,1024]{2,1,0:T(8,128)}, f32[3,1024]{1,0:T(4,128)}, f32[3,1024]{1,0:T(4,128)}, f32[1,1024]{1,0:T(1,128)}, f32[3,3072]{1,0:T(4,128)}) custom-call(f32[19,32,1024]{2,1,0:T(8,128)S(1)} %copy-done, f32[24,1024]{1,0:T(8,128)S(1)} %copy-done.1, s32[1,1024]{1,0:T(1,128)S(1)} %copy-done.5, f32[8,1024]{1,0:T(8,128)S(1)} %copy-done.3, ...), custom_call_target="tpu_custom_call" | custom-call | tf_op jit(solution)/shard_map/finish/pallas_call | solution.py:452
Async XLA Ops:
  0.6 28.5 %copy-start.4 = (s32[2,64]{1,0:T(2,128)S(1)}, s32[2,64]{1,0:T(2,128)}, u32[]{:S(2)}) copy-start(s32[2,64]{1,0:T(2,128)} %mig_ref.3) | copy-start | bytes 1540
  29.1 1.7 %copy-start = (f32[19,32,1024]{2,1,0:T(8,128)S(1)}, f32[19,32,1024]{2,1,0:T(8,128)}, u32[]{:S(2)}) copy-start(f32[19,32,1024]{2,1,0:T(8,128)} %get-tuple-element.16.read_ref) | copy-start | bytes 7471108
  30.8 0.9 %copy-start.1 = (f32[24,1024]{1,0:T(8,128)S(1)}, f32[24,1024]{1,0:T(8,128)}, u32[]{:S(2)}) copy-start(f32[24,1024]{1,0:T(8,128)} %get-tuple-element.17.arrived_ref) | copy-start | bytes 294916
  31.7 0.8 %copy-start.2 = (f32[3,3072]{1,0:T(4,128)S(1)}, f32[3,3072]{1,0:T(4,128)}, u32[]{:S(2)}) copy-start(f32[3,3072]{1,0:T(4,128)} %get-tuple-element.21.spring_ref) | copy-start | bytes 110596
  32.5 0.8 %copy-start.3 = (f32[8,1024]{1,0:T(8,128)S(1)}, f32[8,1024]{1,0:T(8,128)}, u32[]{:S(2)}) copy-start(f32[8,1024]{1,0:T(8,128)} %get-tuple-element.19.state_ref) | copy-start | bytes 98308
  33.3 0.7 %copy-start.5 = (s32[1,1024]{1,0:T(1,128)S(1)}, s32[1,1024]{1,0:T(1,128)}, u32[]{:S(2)}) copy-start(s32[1,1024]{1,0:T(1,128)} %get-tuple-element.18.tgtp_ref) | copy-start | bytes 12292
  33.9 0.7 %copy-start.6 = (f32[8,128]{1,0:T(8,128)S(1)}, f32[8,128]{1,0:T(8,128)}, u32[]{:S(2)}) copy-start(f32[8,128]{1,0:T(8,128)} %get-tuple-element.20.newcomers_ref) | copy-start | bytes 12292
where the time goes:
time: 40.6 us; the launch traced here: 40.2 us
  Pallas kernels  33.3 us (82%)
  local copies, waits for them, and re-layouts  5.5 us (14%)
  between operations  1.33 us (3%)
    pallas_call x1, Pallas kernels, shards(): pl.pallas_call(step_kernel, name='step', out_shape=(jax.ShapeDtypeStruct(...  27.8 us
    pallas_call x1, Pallas kernels, shards(): pl.pallas_call(finish_kernel, name='finish', grid=(4,), out_shape=(jax.Sh...  5.54 us
    unnamed x14, local copies, waits for them, and re-layouts  5.5 us

commit v1 on v0

--- a/solution.py
+++ b/solution.py
@@ -60,12 +60,8 @@
 
 
 def fill_one_hot(ref, row):
-    step = 128
-
-    @pl.loop(0, NYZ // step)
-    def _(i):
-        start = pl.multiple_of(i * step, step)
-        ref[pl.ds(start, step), :] = one_hot(row, step, start)
+    for start in range(0, NYZ, 128):
+        ref[start:start + 128, :] = one_hot(row, 128, start)
 
 
 def dot(a, b, dims):
@@ -126,11 +122,13 @@
 
 
 def step_kernel(
-    pdfs_hbm, flags_hbm, level_ref, pos_ref, vel_ref, rad_ref, cell_ref, pairs_ref, spring_ref, src_ref, off_ref, slot_ref,
-    tgt_ref, mig_ref,
+    pdfs_hbm, flags_hbm, level_ref, pos_hbm, vel_hbm, rad_hbm, cell_hbm, pairs_hbm, spring_hbm, src_hbm, off_hbm, slot_hbm,
+    tgt_hbm, mig_hbm,
     read_ref, arrived_ref, tgtp_ref, state_ref, newcomers_ref, spring_out_ref,
-    pdfs, flags, onehot, moved_in, ext, velf, velb, rows16, edge_x, edge_y, edge_c, halo_x, halo_y, halo_yp, halo_c, splits, gathered,
-    received, leaving, joined, fluid, force,
+    pdfs, flags, pos_ref, vel_ref, rad_ref, cell_ref, pairs_ref, spring_ref, src_ref, off_ref, slot_ref, tgt_ref,
+    mig_ref,
+    onehot, source_hot, moved_in, ext, velf, velb, vel8, rows16, edge_x, edge_y, edge_c, halo_x, halo_y, halo_yp, halo_c, splits,
+    gathered, received, leaving, joined, fluid, force,
     load_sem, send_sem, recv_sem,
 ):
     a, b = lax.axis_index("wide"), lax.axis_index("narrow")
@@ -139,14 +137,23 @@
     def device(dx, dy):
         return (lax.rem(a + dx + n_wide, n_wide), lax.rem(b + dy + n_narrow, n_narrow))
 
-    load_p = pltpu.make_async_copy(pdfs_hbm, pdfs, load_sem.at[0])
-    load_f = pltpu.make_async_copy(flags_hbm, flags, load_sem.at[1])
-    load_p.start()
-    load_f.start()
+    pairs_of = [
+        (cell_hbm, cell_ref), (off_hbm, off_ref), (slot_hbm, slot_ref), (src_hbm, src_ref), (tgt_hbm, tgt_ref),
+        (rad_hbm, rad_ref), (vel_hbm, vel_ref), (mig_hbm, mig_ref), (pdfs_hbm, pdfs),
+        (pairs_hbm, pairs_ref), (pos_hbm, pos_ref), (spring_hbm, spring_ref), (flags_hbm, flags),
+    ]
+    loads = [pltpu.make_async_copy(x, y, load_sem.at[i]) for i, (x, y) in enumerate(pairs_of)]
+    for load in loads:
+        load.start()
     around = [(dx, dy) for dx in (-1, 0, 1) for dy in (-1, 0, 1) if dx or dy] + [(-2, 0), (2, 0)]
     barrier = pltpu.get_barrier_semaphore()
     for dx, dy in around:
         pl.semaphore_signal(barrier, inc=1, device_id=device(dx, dy), device_id_type=MESH)
+    for load in loads[:8]:
+        load.wait()
+
+    src_packed, tgt_packed, counts = pack_interface(off_ref, slot_ref, src_ref, tgt_ref)
+    tgtp_ref[...] = tgt_packed
 
     cell = cell_ref[...]
     grain_x = cell >> 10
@@ -156,25 +163,22 @@
     weights = [drag] + [drag * vel_ref[c:c + 1, :] for c in range(3)]
     for k, weight in enumerate(weights):
         for part, value in enumerate(split2(weight)):
-            moved_in[pl.ds((part * 4 + k) * NX, NX), :] = jnp.where(in_row, value, 0.0).astype(BF16)
-
-    @pl.loop(0, 4)
-    def _(i):
-        cols = pl.ds(pl.multiple_of(i * 256, 256), 256)
+            moved_in[(part * 4 + k) * NX:(part * 4 + k + 1) * NX, :] = jnp.where(in_row, value, 0.0).astype(BF16)
+    fill_one_hot(source_hot, src_packed & 1023)
+
+    fine = level_ref[0, 0] == 1
+    tau = jnp.where(fine, tau_fine, tau_coarse).astype(F32)
+    omega = jnp.where(fine, 1.0 / tau_fine, 1.0 / tau_coarse).astype(F32)
+    keep = jnp.where(fine, 1.0 - 1.0 / tau_fine, 0.0).astype(F32)
+
+    def bring(i):
+        cols = slice(i * 256, (i + 1) * 256)
         got = dot(moved_in[...], onehot[cols, :], NT)
         force[:, cols] = got[0:128] + got[128:256]
 
-    level = level_ref[0, 0]
-    tau = jnp.where(level == 1, tau_fine, tau_coarse).astype(F32)
-    omega = jnp.where(level == 1, 1.0 / tau_fine, 1.0 / tau_coarse).astype(F32)
-    keep = jnp.where(level == 1, 1.0 - 1.0 / tau_fine, 0.0).astype(F32)
-    load_p.wait()
-
-    @pl.loop(0, 32)
-    def _(i):
-        row = pl.multiple_of((i // 8) * 8, 8)
-        rows = pl.ds(row, 8)
-        cols = pl.ds(pl.multiple_of((i % 8) * 128, 128), 128)
+    def collide(row, col):
+        rows = slice(row, row + 8)
+        cols = slice(col, col + 128)
         p = [pdfs[q, rows, cols] for q in range(19)]
         pair_sum = {q: p[q] + p[q + 1] for q in range(1, 19, 2)}
         pair_dif = {q: p[q] - p[q + 1] for q in range(1, 19, 2)}
@@ -187,16 +191,18 @@
         )
         inverse = 1.0 / density
         pull = tau * inverse
-        resist = force[pl.ds(row, 8), cols]
+        resist = force[rows, cols]
         shifted = []
         for c in range(3):
             v = mom[c] * inverse
-            velf[pl.ds(c * NX + row, 8), cols] = v
-            shifted.append(v + pull * (force[pl.ds((c + 1) * NX + row, 8), cols] - v * resist))
+            velf[c * NX + row:c * NX + row + 8, cols] = v
+            shifted.append(v + pull * (force[(c + 1) * NX + row:(c + 1) * NX + row + 8, cols] - v * resist))
         square = 1.5 * (shifted[0] * shifted[0] + shifted[1] * shifted[1] + shifted[2] * shifted[2])
         base = 1.0 - square
         dense = omega * density
-        out_rows = pl.ds(TOP + row, 8)
+        wide = dense * (1.0 / 18.0)
+        slim = dense * (1.0 / 36.0)
+        out_rows = slice(TOP + row, TOP + row + 8)
         ext[0, out_rows, cols] = keep * p[0] + (dense * (1.0 / 3.0)) * base
         for q in range(1, 19, 2):
             along = None
@@ -205,11 +211,20 @@
                     along = shifted[c] if along is None else along + shifted[c]
                 elif VELOCITY[q][c] == -1:
                     along = along - shifted[c]
-            scaled = dense * (1.0 / 18.0 if q < 7 else 1.0 / 36.0)
+            scaled = wide if q < 7 else slim
             even = scaled * (base + 4.5 * along * along)
             odd = scaled * (3.0 * along)
             ext[q, out_rows, cols] = keep * p[q] + (even + odd)
             ext[q + 1, out_rows, cols] = keep * p[q + 1] + (even - odd)
+
+    bring(0)
+    loads[8].wait()
+    for i in range(4):
+        if i < 3:
+            bring(i + 1)
+        for col in (i * 256, i * 256 + 128):
+            for row in range(0, NX, 8):
+                collide(row, col)
 
     for k in range(5):
         edge_x[0, k:k + 1, :] = ext[X_PLUS[k], TOP + NX - 1:TOP + NX, :]
@@ -241,64 +256,17 @@
     ]
 
     for part, value in enumerate(split2(velf[...])):
-        velb[pl.ds(part * 96, 96), :] = value.astype(BF16)
-
-    @pl.loop(0, 4)
-    def _(i):
-        cols = pl.ds(pl.multiple_of(i * 256, 256), 256)
+        velb[part * 96:part * 96 + 96, :] = value.astype(BF16)
+    for i in range(4):
+        cols = slice(i * 256, (i + 1) * 256)
         got = dot(velb[...], onehot[:, cols], NN)
         got = got[0:96] + got[96:192]
         here = iota((NX, 256), 0) == (cell_ref[:, cols] >> 10)
         for c in range(3):
             fluid[c:c + 1, cols] = jnp.sum(jnp.where(here, got[c * NX:(c + 1) * NX], 0.0), axis=0, keepdims=True)
 
-    pair_index = jnp.concatenate([pairs_ref[0:1, :], pairs_ref[1:2, :]], axis=1)
-    pair_high = pair_index >> 7
-    pair_hot = one_hot(pair_index & 127, 128)
-    vel = vel_ref[...]
-    rows16[...] = jnp.zeros_like(rows16)
-    for part, value in enumerate(split3(vel)):
-        rows16[part * 3:part * 3 + 3, 0:NYZ] = value
-    table = jnp.concatenate([rows16[:, h * 128:(h + 1) * 128] for h in range(8)], axis=0).astype(BF16)
-    found = dot(table, pair_hot, NN)
-    at_pair = jnp.where(pair_high == 0, found[0:16], 0.0)
-    for h in range(1, 8):
-        at_pair = jnp.where(pair_high == h, found[h * 16:(h + 1) * 16], at_pair)
-    at_pair = at_pair[0:3] + at_pair[3:6] + at_pair[6:9]
-    relative = at_pair[:, 3072:6144] - at_pair[:, 0:3072]
-    spring = spring_ref[...]
-    spring_out_ref[...] = spring + relative
-    contact = spring_coef * spring + dashpot_coef * relative
-    for part, value in enumerate(split3(contact)):
-        rows16[part * 3:part * 3 + 3, 0:3072] = value
-        rows16[part * 3:part * 3 + 3, 3072:6144] = -value
-    both = rows16[...]
-    spread = jnp.concatenate([jnp.where(pair_high == h, both, 0.0).astype(BF16) for h in range(8)], axis=0)
-    summed = dot(spread, pair_hot, NT)
-    parts = [summed[h * 16:h * 16 + 3] + summed[h * 16 + 3:h * 16 + 6] + summed[h * 16 + 6:h * 16 + 9] for h in range(8)]
-    summed = jnp.concatenate(parts, axis=1)
-    radius = rad_ref[...]
-    total = (drag_coef * radius) * (fluid[0:3, :] - vel) + summed
-    mass = mass_coef * radius * radius * radius
-    falling = jnp.where(iota((3, NYZ), 0) == 2, gravity_z, 0.0)
-    moved_vel = vel + total / mass + falling
-    state_ref[0:3, :] = pos_ref[...] + moved_vel
-    state_ref[3:6, :] = moved_vel
-    state_ref[6:7, :] = radius
-    state_ref[7:8, :] = jnp.ones_like(radius)
-
-    slots = jnp.concatenate([mig_ref[0:1, :], mig_ref[1:2, :]], axis=1)
-    mig_hot = one_hot(slots, NYZ)
-    state = jnp.concatenate(split3(state_ref[...]), axis=0).astype(BF16)
-    out = dot(state, mig_hot, NN)
-    leaving[...] = out[0:8] + out[8:16] + out[16:24]
-    migrate = [send(8, leaving, joined.at[0], -1, 0), send(9, leaving, joined.at[1], 1, 0)]
-
-    src_packed, tgt_packed, counts = pack_interface(off_ref, slot_ref, src_ref, tgt_ref)
-    tgtp_ref[...] = tgt_packed
-    fill_one_hot(onehot, src_packed & 1023)
-
-    load_f.wait()
+    for load in loads[9:]:
+        load.wait()
     for copy in halo:
         copy.wait()
     for k in range(5):
@@ -331,18 +299,90 @@
             value = jnp.where(solid, ext[OPPOSITE[q], TOP:TOP + NX, :], value)
         read_ref[q] = value
         high, low = split2(value)
-        splits[pl.ds(q * NX, NX), :] = high.astype(BF16)
-        splits[pl.ds((19 + q) * NX, NX), :] = low.astype(BF16)
-
-    rows_out = []
-    for i in range(4):
+        splits[q * NX:q * NX + NX, :] = high.astype(BF16)
+        splits[(19 + q) * NX:(19 + q) * NX + NX, :] = low.astype(BF16)
+
+    def extract(i):
         cols = slice(i * 256, (i + 1) * 256)
-        got = dot(splits[...], onehot[:, cols], NN)
+        got = dot(splits[...], source_hot[:, cols], NN)
         here = iota((NX, 256), 0) == (src_packed[:, cols] >> 10)
         for q in range(19):
             both_parts = got[q * NX:(q + 1) * NX] + got[(19 + q) * NX:(20 + q) * NX]
             gathered[i, q:q + 1, :] = jnp.sum(jnp.where(here, both_parts, 0.0), axis=0, keepdims=True)
+
+    def contacts_in():
+        vel8[...] = jnp.zeros_like(vel8)
+        vel8[0:3, :] = vel_ref[...]
+        vel8[4:7, :] = vel_ref[...]
+        tables = [vel8[:, h * 128:(h + 1) * 128] for h in range(8)]
+        half = iota((8, 128), 0) < 4
+        for c in range(24):
+            cols = slice(c * 128, (c + 1) * 128)
+            index = jnp.where(half, pairs_ref[0:1, cols], pairs_ref[1:2, cols])
+            low = index & 127
+            high = index >> 7
+            found = jnp.take_along_axis(tables[0], low, axis=1, mode="promise_in_bounds")
+            for h in range(1, 8):
+                found = jnp.where(high == h, jnp.take_along_axis(tables[h], low, axis=1, mode="promise_in_bounds"), found)
+            relative = found[4:7] - found[0:3]
+            spring = spring_ref[:, cols]
+            spring_out_ref[:, cols] = spring + relative
+            contact = spring_coef * spring + dashpot_coef * relative
+            for part, value in enumerate(split3(contact)):
+                rows16[part * 3:part * 3 + 3, cols] = value
+
+    def contacts_out():
+        rows16[9:16, :] = jnp.zeros((7, 3072), F32)
+        forces = rows16[...]
+        spread = []
+        hots = []
+        for side in range(2):
+            index = pairs_ref[side:side + 1, :]
+            high = index >> 7
+            signed = -forces if side else forces
+            spread.append(jnp.concatenate([jnp.where(high == h, signed, 0.0).astype(BF16) for h in range(8)], axis=0))
+            hots.append(one_hot(index & 127, 128))
+        summed = dot(jnp.concatenate(spread, axis=1), jnp.concatenate(hots, axis=1), NT)
+        parts = [
+            summed[h * 16:h * 16 + 3] + summed[h * 16 + 3:h * 16 + 6] + summed[h * 16 + 6:h * 16 + 9] for h in range(8)]
+        return jnp.concatenate(parts, axis=1)
+
+    def move_grains(summed):
+        radius = rad_ref[...]
+        vel = vel_ref[...]
+        total = (drag_coef * radius) * (fluid[0:3, :] - vel) + summed
+        mass = mass_coef * radius * radius * radius
+        falling = jnp.where(iota((3, NYZ), 0) == 2, gravity_z, 0.0)
+        moved_vel = vel + total / mass + falling
+        state_ref[0:3, :] = pos_ref[...] + moved_vel
+        state_ref[3:6, :] = moved_vel
+        state_ref[6:7, :] = radius
+        state_ref[7:8, :] = jnp.ones_like(radius)
+
+    def leave():
+        slots = jnp.concatenate([mig_ref[0:1, :], mig_ref[1:2, :]], axis=1)
+        state = jnp.concatenate(split3(state_ref[...]), axis=0).astype(BF16)
+        out = dot(state, one_hot(slots, NYZ), NN)
+        leaving[...] = out[0:8] + out[8:16] + out[16:24]
+
+    rows_out = []
+
+    def send_region(i):
         rows_out.append(send(10 + i, gathered.at[i], received.at[i], DISTANCE[i], 0))
+
+    extract(0)
+    contacts_in()
+    send_region(0)
+    extract(1)
+    summed = contacts_out()
+    send_region(1)
+    extract(2)
+    move_grains(summed)
+    leave()
+    migrate = [send(8, leaving, joined.at[0], -1, 0), send(9, leaving, joined.at[1], 1, 0)]
+    send_region(2)
+    extract(3)
+    send_region(3)
 
     for copy in migrate:
         copy.wait()
@@ -381,11 +421,12 @@
         rad_ref[...] = result[6:7]
         spring_out_ref[...] = spring_ref[...]
 
+    cols = pl.ds(pl.multiple_of(step * 256, 256), 256)
     hot = one_hot(target & 1023, 256, step * 256)
     got = dot(spread[...], hot, NT)
     hit = got[38 * NX:39 * NX] > 0.5
     for q in range(19):
-        value = read_ref[q]
+        value = read_ref[q, :, cols]
         carried = got[q * NX:(q + 1) * NX] + got[(19 + q) * NX:(20 + q) * NX]
         next_ref[q] = jnp.where(hit, blend_coef * (value + carried), value)
 
@@ -401,24 +442,37 @@
         step_kernel,
         name="step",
         out_shape=(
-            jax.ShapeDtypeStruct((19, NX, NYZ), F32),
-            jax.ShapeDtypeStruct((24, NYZ), F32),
-            jax.ShapeDtypeStruct(row, jnp.int32),
-            jax.ShapeDtypeStruct((8, NYZ), F32),
-            jax.ShapeDtypeStruct((8, 128), F32),
-            jax.ShapeDtypeStruct((3, 3072), F32),
+            pltpu.VMEM((19, NX, NYZ), F32),
+            pltpu.VMEM((24, NYZ), F32),
+            pltpu.VMEM(row, jnp.int32),
+            pltpu.VMEM((8, NYZ), F32),
+            pltpu.VMEM((8, 128), F32),
+            pltpu.VMEM((3, 3072), F32),
         ),
-        in_specs=[hbm, hbm, pl.BlockSpec(memory_space=pltpu.SMEM)] + [vmem] * 11,
+        in_specs=[hbm] * 2 + [pl.BlockSpec(memory_space=pltpu.SMEM)] + [hbm] * 11,
         out_specs=(vmem,) * 6,
         scratch_shapes=[
             pltpu.VMEM((19, NX, NYZ), F32),
             pltpu.VMEM((2, NX, NYZ), jnp.int32),
+            pltpu.VMEM((3, NYZ), F32),
+            pltpu.VMEM((3, NYZ), F32),
+            pltpu.VMEM(row, F32),
+            pltpu.VMEM(row, jnp.int32),
+            pltpu.VMEM((2, 3072), jnp.int32),
+            pltpu.VMEM((3, 3072), F32),
+            pltpu.VMEM(row, jnp.int32),
+            pltpu.VMEM(row, jnp.int32),
+            pltpu.VMEM(row, jnp.int32),
+            pltpu.VMEM((8, 128), jnp.int32),
+            pltpu.VMEM((2, 64), jnp.int32),
+            pltpu.VMEM((NYZ, NYZ), BF16),
             pltpu.VMEM((NYZ, NYZ), BF16),
             pltpu.VMEM((8 * NX, NYZ), BF16),
             pltpu.VMEM((19, EXT, NYZ), F32),
             pltpu.VMEM((3 * NX, NYZ), F32),
             pltpu.VMEM((6 * NX, NYZ), BF16),
-            pltpu.VMEM((16, 6144), F32),
+            pltpu.VMEM((8, NYZ), F32),
+            pltpu.VMEM((16, 3072), F32),
             pltpu.VMEM((2, 8, NYZ), F32),
             pltpu.VMEM((2, 5, NX, 128), F32),
             pltpu.VMEM((4, 8, 128), F32),
@@ -433,11 +487,11 @@
             pltpu.VMEM((2, 8, 128), F32),
             pltpu.VMEM((8, NYZ), F32),
             pltpu.VMEM((4 * NX, NYZ), F32),
-            pltpu.SemaphoreType.DMA((2,)),
+            pltpu.SemaphoreType.DMA((14,)),
             pltpu.SemaphoreType.DMA((14,)),
             pltpu.SemaphoreType.DMA((14,)),
         ],
-        compiler_params=pltpu.CompilerParams(collective_id=0, has_side_effects=True, vmem_limit_bytes=56 << 20),
+        compiler_params=pltpu.CompilerParams(collective_id=0, has_side_effects=True, vmem_limit_bytes=64_300_000),
     )(
         pdfs, link_flags, block_level, grain_pos, grain_vel, grain_radius.reshape(row), grain_cell.reshape(row), contact_pairs,
         contact_spring, iface_source.reshape(row), iface_offset.reshape(row), iface_slot.reshape(row),
@@ -460,7 +514,7 @@
             jax.ShapeDtypeStruct(row, F32),
             jax.ShapeDtypeStruct((3, 3072), F32),
         ),
-        in_specs=[block, whole((24, NYZ)), whole(row), whole((8, NYZ)), whole((8, 128)), whole((2, 64)), whole((3, 3072))],
+        in_specs=[vmem] * 7,
         out_specs=(block, whole((3, NYZ)), whole((3, NYZ)), whole(row), whole((3, 3072))),
         scratch_shapes=[pltpu.VMEM((39 * NX, NYZ), BF16)],
         compiler_params=pltpu.CompilerParams(dimension_semantics=("arbitrary",), vmem_limit_bytes=40 << 20),

time: 40.6 us -> 30.9 us (0.76)
  local copies, waits for them, and re-layouts: 5.5 us -> 0.01 us
  Pallas kernels: 33.3 us -> 29.4 us
    unnamed x14 -> x2, local copies, waits for them, and re-layouts: 5.5 us -> 0.01 us
    pallas_call x1, Pallas kernels: 27.8 us -> 24.1 us  [shards(): pl.pallas_call(step_kernel, name='step', out_shape=(pltpu.VMEM((19, NX, N...]
where the time goes in v1:
time: 30.9 us; the launch traced here: 30.8 us
  Pallas kernels  29.4 us (95%)
  between operations  1.32 us (4%)
    pallas_call x1, Pallas kernels, shards(): pl.pallas_call(step_kernel, name='step', out_shape=(pltpu.VMEM((19, NX, N...  24.1 us
    pallas_call x1, Pallas kernels, shards(): pl.pallas_call(finish_kernel, name='finish', grid=(4,), out_shape=(jax.Sh...  5.37 us

profile of v1, /device:TPU:1, one launch (start us, length us, event | category | flops | bytes accessed | tf_op | source)
XLA Modules:
  0.0 30.8 jit_solution(4810670869709303711)
XLA Ops:
  0.6 0.0 copy-start
  1.3 24.1 %step.1 = (f32[19,32,1024]{2,1,0:T(8,128)S(1)}, f32[24,1024]{1,0:T(8,128)S(1)}, s32[1,1024]{1,0:T(1,128)S(1)}, f32[8,1024]{1,0:T(8,128)S(1)}, f32[8,128]{1,0:T(8,128)S(1)}, /*index=5*/f32[3,3072]{1,0:T(4,128)S(1)}) custom-call(f32[19,32,1024]{2,1,0:T(8,128)} %pdfs_hbm.1, s32[2,32,1024]{2,1,0:T(8,128)} %flags_hbm.1, s32[1,1]{1,0:T(1,128)S(6)} %copy.19.level_ref, ...), custom_call_target="tpu_custom_call" | custom-call | tf_op jit(solution)/shard_map/step/pallas_call | solution.py:441
  25.4 0.0 copy-done
  25.4 5.4 %finish.1 = (f32[19,32,1024]{2,1,0:T(8,128)}, f32[3,1024]{1,0:T(4,128)}, f32[3,1024]{1,0:T(4,128)}, f32[1,1024]{1,0:T(1,128)}, f32[3,3072]{1,0:T(4,128)}) custom-call(f32[19,32,1024]{2,1,0:T(8,128)S(1)} %get-tuple-element.16.read_ref, f32[24,1024]{1,0:T(8,128)S(1)} %get-tuple-element.17.arrived_ref, s32[1,1024]{1,0:T(1,128)S(1)} %get-tuple-element.18.tgtp_ref, ...), custom_call_target="tpu_custom_call" | custom-call | tf_op jit(solution)/shard_map/finish/pallas_call | solution.py:506
Async XLA Ops:
  0.6 24.7 %copy-start = (s32[2,64]{1,0:T(2,128)S(1)}, s32[2,64]{1,0:T(2,128)}, u32[]{:S(2)}) copy-start(s32[2,64]{1,0:T(2,128)} %mig_ref.1) | copy-start | bytes 1540

commit v2 on v1

--- a/solution.py
+++ b/solution.py
@@ -22,6 +22,9 @@
 gravity_z = -0.01
 blend_coef = 0.5
 
+ROOT2 = 1.4142135623730951
+THREE_BY_ROOT2 = 2.1213203435596424
+GROUPS = (tuple(range(19)), ())
 NX = 32
 NYZ = 1024
 TOP = 8
@@ -124,7 +127,7 @@
 def step_kernel(
     pdfs_hbm, flags_hbm, level_ref, pos_hbm, vel_hbm, rad_hbm, cell_hbm, pairs_hbm, spring_hbm, src_hbm, off_hbm, slot_hbm,
     tgt_hbm, mig_hbm,
-    read_ref, arrived_ref, tgtp_ref, state_ref, newcomers_ref, spring_out_ref,
+    read_ref, spread_ref, tgtp_ref, state_ref, newcomers_ref, spring_out_ref,
     pdfs, flags, pos_ref, vel_ref, rad_ref, cell_ref, pairs_ref, spring_ref, src_ref, off_ref, slot_ref, tgt_ref,
     mig_ref,
     onehot, source_hot, moved_in, ext, velf, velb, vel8, rows16, edge_x, edge_y, edge_c, halo_x, halo_y, halo_yp, halo_c, splits,
@@ -172,7 +175,7 @@
     keep = jnp.where(fine, 1.0 - 1.0 / tau_fine, 0.0).astype(F32)
 
     def bring(i):
-        cols = slice(i * 256, (i + 1) * 256)
+        cols = slice(i * 512, (i + 1) * 512)
         got = dot(moved_in[...], onehot[cols, :], NT)
         force[:, cols] = got[0:128] + got[128:256]
 
@@ -196,14 +199,15 @@
         for c in range(3):
             v = mom[c] * inverse
             velf[c * NX + row:c * NX + row + 8, cols] = v
-            shifted.append(v + pull * (force[(c + 1) * NX + row:(c + 1) * NX + row + 8, cols] - v * resist))
-        square = 1.5 * (shifted[0] * shifted[0] + shifted[1] * shifted[1] + shifted[2] * shifted[2])
-        base = 1.0 - square
+            shifted.append(THREE_BY_ROOT2 * (v + pull * (force[(c + 1) * NX + row:(c + 1) * NX + row + 8, cols] - v * resist)))
+        base = 1.0 - (shifted[0] * shifted[0] + shifted[1] * shifted[1] + shifted[2] * shifted[2]) * (1.0 / 3.0)
         dense = omega * density
-        wide = dense * (1.0 / 18.0)
         slim = dense * (1.0 / 36.0)
+        wide = slim + slim
+        slim_base = slim * base
+        wide_base = slim_base + slim_base
         out_rows = slice(TOP + row, TOP + row + 8)
-        ext[0, out_rows, cols] = keep * p[0] + (dense * (1.0 / 3.0)) * base
+        ext[0, out_rows, cols] = keep * p[0] + 6.0 * wide_base
         for q in range(1, 19, 2):
             along = None
             for c in range(3):
@@ -211,18 +215,18 @@
                     along = shifted[c] if along is None else along + shifted[c]
                 elif VELOCITY[q][c] == -1:
                     along = along - shifted[c]
-            scaled = wide if q < 7 else slim
-            even = scaled * (base + 4.5 * along * along)
-            odd = scaled * (3.0 * along)
+            scaled = (wide if q < 7 else slim) * along
+            even = (wide_base if q < 7 else slim_base) + scaled * along
+            odd = ROOT2 * scaled
             ext[q, out_rows, cols] = keep * p[q] + (even + odd)
             ext[q + 1, out_rows, cols] = keep * p[q + 1] + (even - odd)
 
     bring(0)
     loads[8].wait()
-    for i in range(4):
-        if i < 3:
+    for i in range(2):
+        if i < 1:
             bring(i + 1)
-        for col in (i * 256, i * 256 + 128):
+        for col in range(i * 512, i * 512 + 512, 128):
             for row in range(0, NX, 8):
                 collide(row, col)
 
@@ -255,60 +259,53 @@
         send(7, edge_c.at[3], halo_c.at[3], -1, 1),
     ]
 
-    for part, value in enumerate(split2(velf[...])):
-        velb[part * 96:part * 96 + 96, :] = value.astype(BF16)
-    for i in range(4):
-        cols = slice(i * 256, (i + 1) * 256)
-        got = dot(velb[...], onehot[:, cols], NN)
-        got = got[0:96] + got[96:192]
-        here = iota((NX, 256), 0) == (cell_ref[:, cols] >> 10)
-        for c in range(3):
-            fluid[c:c + 1, cols] = jnp.sum(jnp.where(here, got[c * NX:(c + 1) * NX], 0.0), axis=0, keepdims=True)
-
-    for load in loads[9:]:
-        load.wait()
-    for copy in halo:
-        copy.wait()
-    for k in range(5):
-        ext[X_PLUS[k], TOP - 1:TOP, :] = halo_x[0, k:k + 1, :]
-        ext[X_MINUS[k], TOP + NX:TOP + NX + 1, :] = halo_x[1, k:k + 1, :]
-        for side in range(2):
-            halo_yp[side, k, TOP:TOP + NX, :] = halo_y[side, k]
-    halo_yp[0, 1, TOP - 1:TOP, :] = halo_c[0, 0:1, :]
-    halo_yp[1, 1, TOP + NX:TOP + NX + 1, :] = halo_c[1, 0:1, :]
-    halo_yp[1, 2, TOP - 1:TOP, :] = halo_c[2, 0:1, :]
-    halo_yp[0, 2, TOP + NX:TOP + NX + 1, :] = halo_c[3, 0:1, :]
+    def fluid_at_grains():
+        for part, value in enumerate(split2(velf[...])):
+            velb[part * 96:part * 96 + 96, :] = value.astype(BF16)
+        for i in range(2):
+            cols = slice(i * 512, (i + 1) * 512)
+            got = dot(velb[...], onehot[:, cols], NN)
+            got = got[0:96] + got[96:192]
+            here = iota((NX, 512), 0) == (cell_ref[:, cols] >> 10)
+            for c in range(3):
+                fluid[c:c + 1, cols] = jnp.sum(jnp.where(here, got[c * NX:(c + 1) * NX], 0.0), axis=0, keepdims=True)
+
     lane = iota((NX, 128), 1)
-    for q in range(19):
-        cx, cy, cz = VELOCITY[q]
-        shift = cy * 32 + cz
-        rows = slice(TOP - cx, TOP - cx + NX)
-        value = ext[q, rows, :]
-        if shift:
-            value = pltpu.roll(value, shift % NYZ, 1)
-        if cy == 1:
-            edge = pltpu.roll(halo_yp[0, Y_PLUS.index(q), rows, :], shift % 128, 1)
-            value = jnp.concatenate([jnp.where(lane < 32, edge, value[:, 0:128]), value[:, 128:]], axis=1)
-        if cy == -1:
-            edge = halo_yp[1, Y_MINUS.index(q), rows, :]
-            edge = pltpu.roll(edge, shift % 128, 1)
-            value = jnp.concatenate([value[:, :896], jnp.where(lane >= 96, edge, value[:, 896:])], axis=1)
-        if q:
-            bit = 1 << (q if q < 10 else q - 10)
-            solid = (flags[0 if q < 10 else 1] & bit) != 0
-            value = jnp.where(solid, ext[OPPOSITE[q], TOP:TOP + NX, :], value)
-        read_ref[q] = value
-        high, low = split2(value)
-        splits[q * NX:q * NX + NX, :] = high.astype(BF16)
-        splits[(19 + q) * NX:(19 + q) * NX + NX, :] = low.astype(BF16)
-
-    def extract(i):
-        cols = slice(i * 256, (i + 1) * 256)
-        got = dot(splits[...], source_hot[:, cols], NN)
-        here = iota((NX, 256), 0) == (src_packed[:, cols] >> 10)
-        for q in range(19):
-            both_parts = got[q * NX:(q + 1) * NX] + got[(19 + q) * NX:(20 + q) * NX]
-            gathered[i, q:q + 1, :] = jnp.sum(jnp.where(here, both_parts, 0.0), axis=0, keepdims=True)
+
+    def stream(group):
+        for k, q in enumerate(group):
+            cx, cy, cz = VELOCITY[q]
+            shift = cy * 32 + cz
+            rows = slice(TOP - cx, TOP - cx + NX)
+            value = ext[q, rows, :]
+            if shift:
+                value = pltpu.roll(value, shift % NYZ, 1)
+            if cy == 1:
+                edge = pltpu.roll(halo_yp[0, Y_PLUS.index(q), rows, :], shift % 128, 1)
+                value = jnp.concatenate([jnp.where(lane < 32, edge, value[:, 0:128]), value[:, 128:]], axis=1)
+            if cy == -1:
+                edge = pltpu.roll(halo_yp[1, Y_MINUS.index(q), rows, :], shift % 128, 1)
+                value = jnp.concatenate([value[:, :896], jnp.where(lane >= 96, edge, value[:, 896:])], axis=1)
+            if q:
+                bit = 1 << (q if q < 10 else q - 10)
+                solid = (flags[0 if q < 10 else 1] & bit) != 0
+                value = jnp.where(solid, ext[OPPOSITE[q], TOP:TOP + NX, :], value)
+            read_ref[q] = value
+            high, low = split2(value)
+            at = group[0] * 2 * NX + k * NX
+            splits[at:at + NX, :] = high.astype(BF16)
+            splits[at + len(group) * NX:at + (len(group) + 1) * NX, :] = low.astype(BF16)
+
+    def extract(group, i, width=1):
+        cols = slice(i * 256, (i + width) * 256)
+        at, size = group[0] * 2 * NX, len(group) * NX
+        got = dot(splits[at:at + 2 * size, :], source_hot[:, cols], NN)
+        here = iota((NX, 256 * width), 0) == (src_packed[:, cols] >> 10)
+        for k, q in enumerate(group):
+            value = got[k * NX:(k + 1) * NX] + got[size + k * NX:size + (k + 1) * NX]
+            value = jnp.sum(jnp.where(here, value, 0.0), axis=0, keepdims=True)
+            for w in range(width):
+                gathered[i + w, q:q + 1, :] = value[:, w * 256:(w + 1) * 256]
 
     def contacts_in():
         vel8[...] = jnp.zeros_like(vel8)
@@ -370,18 +367,31 @@
     def send_region(i):
         rows_out.append(send(10 + i, gathered.at[i], received.at[i], DISTANCE[i], 0))
 
-    extract(0)
+    for load in loads[9:]:
+        load.wait()
+    for copy in halo:
+        copy.wait()
+    for k in range(5):
+        ext[X_PLUS[k], TOP - 1:TOP, :] = halo_x[0, k:k + 1, :]
+        ext[X_MINUS[k], TOP + NX:TOP + NX + 1, :] = halo_x[1, k:k + 1, :]
+        for side in range(2):
+            halo_yp[side, k, TOP:TOP + NX, :] = halo_y[side, k]
+    halo_yp[0, 1, TOP - 1:TOP, :] = halo_c[0, 0:1, :]
+    halo_yp[1, 1, TOP + NX:TOP + NX + 1, :] = halo_c[1, 0:1, :]
+    halo_yp[1, 2, TOP - 1:TOP, :] = halo_c[2, 0:1, :]
+    halo_yp[0, 2, TOP + NX:TOP + NX + 1, :] = halo_c[3, 0:1, :]
+    stream(GROUPS[0])
+    fluid_at_grains()
+    extract(GROUPS[0], 0, 2)
     contacts_in()
+    summed = contacts_out()
     send_region(0)
-    extract(1)
-    summed = contacts_out()
     send_region(1)
-    extract(2)
+    extract(GROUPS[0], 2, 2)
     move_grains(summed)
     leave()
     migrate = [send(8, leaving, joined.at[0], -1, 0), send(9, leaving, joined.at[1], 1, 0)]
     send_region(2)
-    extract(3)
     send_region(3)
 
     for copy in migrate:
@@ -389,46 +399,54 @@
     mig_lane = iota((8, 128), 1)
     change = jnp.where(iota((8, 128), 0) == 0, jnp.where(mig_lane < 64, float(NX), -float(NX)), 0.0)
     newcomers_ref[...] = jnp.where(mig_lane < 64, joined[0], joined[1]) + change
+
     for i in range(4):
+        cols = slice(i * 256, (i + 1) * 256)
         rows_out[i].wait()
         stays = iota((24, 256), 1).astype(F32) >= counts[i]
-        arrived_ref[:, i * 256:(i + 1) * 256] = jnp.where(stays, gathered[i], received[i])
+        carried = jnp.where(stays, gathered[i], received[i])
+        here = iota((NX, 256), 0) == (tgt_packed[:, cols] >> 10)
+        for q in range(19):
+            for part, value in enumerate(split2(carried[q:q + 1, :])):
+                spread_ref[(part * 19 + q) * NX:(part * 19 + q + 1) * NX, cols] = jnp.where(here, value, 0.0).astype(BF16)
+        spread_ref[38 * NX:39 * NX, cols] = jnp.where(here, 1.0, 0.0).astype(BF16)
 
 
 def finish_kernel(
-    read_ref, arrived_ref, tgtp_ref, state_ref, newcomers_ref, mig_ref, spring_ref,
-    next_ref, pos_ref, vel_ref, rad_ref, spring_out_ref,
-    spread,
+    read_ref, spread_ref, tgtp_ref, state_ref, newcomers_ref, mig_ref, spring_ref,
+    next_hbm, pos_hbm, vel_hbm, rad_hbm, spring_hbm,
+    blended, pos, vel, rad, sem,
 ):
-    step = pl.program_id(0)
-    target = tgtp_ref[...]
-
-    @pl.when(step == 0)
-    def _():
-        here = iota((NX, NYZ), 0) == (target >> 10)
-        for q in range(19):
-            for part, value in enumerate(split2(arrived_ref[q:q + 1, :])):
-                spread[pl.ds((part * 19 + q) * NX, NX), :] = jnp.where(here, value, 0.0).astype(BF16)
-        spread[pl.ds(38 * NX, NX), :] = jnp.where(here, 1.0, 0.0).astype(BF16)
-        slots = jnp.concatenate([mig_ref[0:1, :], mig_ref[1:2, :]], axis=1)
-        mig_hot = one_hot(slots, NYZ)
-        arrived = jnp.concatenate(split3(newcomers_ref[...]), axis=0).astype(BF16)
-        placed = dot(arrived, mig_hot, NT)
-        placed = placed[0:8] + placed[8:16] + placed[16:24]
-        result = jnp.where(placed[7:8] > 0.5, placed, state_ref[...])
-        pos_ref[...] = result[0:3]
-        vel_ref[...] = result[3:6]
-        rad_ref[...] = result[6:7]
-        spring_out_ref[...] = spring_ref[...]
-
-    cols = pl.ds(pl.multiple_of(step * 256, 256), 256)
-    hot = one_hot(target & 1023, 256, step * 256)
-    got = dot(spread[...], hot, NT)
-    hit = got[38 * NX:39 * NX] > 0.5
-    for q in range(19):
-        value = read_ref[q, :, cols]
-        carried = got[q * NX:(q + 1) * NX] + got[(19 + q) * NX:(20 + q) * NX]
-        next_ref[q] = jnp.where(hit, blend_coef * (value + carried), value)
+    copies = [pltpu.make_async_copy(spring_ref, spring_hbm, sem.at[0])]
+    copies[0].start()
+
+    slots = jnp.concatenate([mig_ref[0:1, :], mig_ref[1:2, :]], axis=1)
+    arrived = jnp.concatenate(split3(newcomers_ref[...]), axis=0).astype(BF16)
+    placed = dot(arrived, one_hot(slots, NYZ), NT)
+    placed = placed[0:8] + placed[8:16] + placed[16:24]
+    result = jnp.where(placed[7:8] > 0.5, placed, state_ref[...])
+    pos[...] = result[0:3]
+    vel[...] = result[3:6]
+    rad[...] = result[6:7]
+    for source, target in ((pos, pos_hbm), (vel, vel_hbm), (rad, rad_hbm)):
+        copies.append(pltpu.make_async_copy(source, target, sem.at[len(copies)]))
+        copies[-1].start()
+
+    row = tgtp_ref[...] & 1023
+    for i in range(4):
+        cols = slice(i * 256, (i + 1) * 256)
+        got = dot(spread_ref[...], one_hot(row, 256, i * 256), NT)
+        hit = got[38 * NX:39 * NX] > 0.5
+        for start, stop in ((0, 10), (10, 19)):
+            for q in range(start, stop):
+                value = read_ref[q, :, cols]
+                carried = got[q * NX:(q + 1) * NX] + got[(19 + q) * NX:(20 + q) * NX]
+                blended[q, :, cols] = jnp.where(hit, blend_coef * (value + carried), value)
+            copies.append(pltpu.make_async_copy(
+                blended.at[start:stop, :, cols], next_hbm.at[start:stop, :, cols], sem.at[len(copies)]))
+            copies[-1].start()
+    for copy in copies:
+        copy.wait()
 
 
 def shards(
@@ -443,7 +461,7 @@
         name="step",
         out_shape=(
             pltpu.VMEM((19, NX, NYZ), F32),
-            pltpu.VMEM((24, NYZ), F32),
+            pltpu.VMEM((39 * NX, NYZ), BF16),
             pltpu.VMEM(row, jnp.int32),
             pltpu.VMEM((8, NYZ), F32),
             pltpu.VMEM((8, 128), F32),
@@ -491,22 +509,16 @@
             pltpu.SemaphoreType.DMA((14,)),
             pltpu.SemaphoreType.DMA((14,)),
         ],
-        compiler_params=pltpu.CompilerParams(collective_id=0, has_side_effects=True, vmem_limit_bytes=64_300_000),
+        compiler_params=pltpu.CompilerParams(collective_id=0, has_side_effects=True, vmem_limit_bytes=61_800_000),
     )(
         pdfs, link_flags, block_level, grain_pos, grain_vel, grain_radius.reshape(row), grain_cell.reshape(row), contact_pairs,
         contact_spring, iface_source.reshape(row), iface_offset.reshape(row), iface_slot.reshape(row),
         iface_target.reshape(8, 128), migrant_slots,
     )
-    read, arrived, tgtp, state, newcomers, spring_next = outs
-
-    def whole(shape):
-        return pl.BlockSpec(shape, lambda i: (0,) * len(shape))
-
-    block = pl.BlockSpec((19, NX, 256), lambda i: (0, 0, i))
+    read, spread, tgtp, state, newcomers, spring_next = outs
     result = pl.pallas_call(
         finish_kernel,
         name="finish",
-        grid=(4,),
         out_shape=(
             jax.ShapeDtypeStruct((19, NX, NYZ), F32),
             jax.ShapeDtypeStruct((3, NYZ), F32),
@@ -515,10 +527,16 @@
             jax.ShapeDtypeStruct((3, 3072), F32),
         ),
         in_specs=[vmem] * 7,
-        out_specs=(block, whole((3, NYZ)), whole((3, NYZ)), whole(row), whole((3, 3072))),
-        scratch_shapes=[pltpu.VMEM((39 * NX, NYZ), BF16)],
-        compiler_params=pltpu.CompilerParams(dimension_semantics=("arbitrary",), vmem_limit_bytes=40 << 20),
-    )(read, arrived, tgtp, state, newcomers, migrant_slots, spring_next)
+        out_specs=(hbm,) * 5,
+        scratch_shapes=[
+            pltpu.VMEM((19, NX, NYZ), F32),
+            pltpu.VMEM((3, NYZ), F32),
+            pltpu.VMEM((3, NYZ), F32),
+            pltpu.VMEM(row, F32),
+            pltpu.SemaphoreType.DMA((12,)),
+        ],
+        compiler_params=pltpu.CompilerParams(vmem_limit_bytes=40 << 20),
+    )(read, spread, tgtp, state, newcomers, migrant_slots, spring_next)
     pdfs_next, pos_next, vel_next, rad_next, spring_out = result
     return pdfs_next, pos_next, vel_next, rad_next.reshape(NYZ), spring_out
 

time: 30.9 us -> 30 us (0.971)
  Pallas kernels: 29.4 us -> 28.5 us
    pallas_call x1, Pallas kernels: 5.37 us -> 4.57 us  [shards(): pl.pallas_call(finish_kernel, name='finish', out_shape=(jax.ShapeDtypeStr...]
where the time goes in v2:
time: 30 us; the launch traced here: 29.9 us
  Pallas kernels  28.5 us (95%)
  between operations  1.32 us (4%)
    pallas_call x1, Pallas kernels, shards(): pl.pallas_call(step_kernel, name='step', out_shape=(pltpu.VMEM((19, NX, N...  24 us
    pallas_call x1, Pallas kernels, shards(): pl.pallas_call(finish_kernel, name='finish', out_shape=(jax.ShapeDtypeStr...  4.57 us

profile of v2, /device:TPU:1, one launch (start us, length us, event | category | flops | bytes accessed | tf_op | source)
XLA Modules:
  0.0 29.9 jit_solution(4509634240832267451)
XLA Ops:
  0.6 0.0 copy-start
  1.3 24.0 %step.1 = (f32[19,32,1024]{2,1,0:T(8,128)S(1)}, bf16[1248,1024]{1,0:T(8,128)(2,1)S(1)}, s32[1,1024]{1,0:T(1,128)S(1)}, f32[8,1024]{1,0:T(8,128)S(1)}, f32[8,128]{1,0:T(8,128)S(1)}, /*index=5*/f32[3,3072]{1,0:T(4,128)S(1)}) custom-call(f32[19,32,1024]{2,1,0:T(8,128)} %pdfs_hbm.1, s32[2,32,1024]{2,1,0:T(8,128)} %flags_hbm.1, s32[1,1]{1,0:T(1,128)S(6)} %copy.19.level_ref, ...), custom_call_target="tpu_custom_call" | custom-call | tf_op jit(solution)/shard_map/step/pallas_call | solution.py:459
  25.3 0.0 copy-done
  25.3 4.6 %finish.1 = (f32[19,32,1024]{2,1,0:T(8,128)}, f32[3,1024]{1,0:T(4,128)}, f32[3,1024]{1,0:T(4,128)}, f32[1,1024]{1,0:T(1,128)}, f32[3,3072]{1,0:T(4,128)}) custom-call(f32[19,32,1024]{2,1,0:T(8,128)S(1)} %get-tuple-element.16.read_ref, bf16[1248,1024]{1,0:T(8,128)(2,1)S(1)} %get-tuple-element.17.spread_ref, s32[1,1024]{1,0:T(1,128)S(1)} %get-tuple-element.18.tgtp_ref, ...), custom_call_target="tpu_custom_call" | custom-call | tf_op jit(solution)/shard_map/finish/pallas_call | solution.py:519
Async XLA Ops:
  0.6 24.7 %copy-start = (s32[2,64]{1,0:T(2,128)S(1)}, s32[2,64]{1,0:T(2,128)}, u32[]{:S(2)}) copy-start(s32[2,64]{1,0:T(2,128)} %mig_ref.1) | copy-start | bytes 1540

commit v3 on v2

--- a/solution.py
+++ b/solution.py
@@ -127,11 +127,11 @@
 def step_kernel(
     pdfs_hbm, flags_hbm, level_ref, pos_hbm, vel_hbm, rad_hbm, cell_hbm, pairs_hbm, spring_hbm, src_hbm, off_hbm, slot_hbm,
     tgt_hbm, mig_hbm,
-    read_ref, spread_ref, tgtp_ref, state_ref, newcomers_ref, spring_out_ref,
+    read_ref, spread_ref, tgtp_ref, result_ref, spring_out_ref,
     pdfs, flags, pos_ref, vel_ref, rad_ref, cell_ref, pairs_ref, spring_ref, src_ref, off_ref, slot_ref, tgt_ref,
     mig_ref,
     onehot, source_hot, moved_in, ext, velf, velb, vel8, rows16, edge_x, edge_y, edge_c, halo_x, halo_y, halo_yp, halo_c, splits,
-    gathered, received, leaving, joined, fluid, force,
+    gathered, received, leaving, joined, fluid, force, state_ref,
     load_sem, send_sem, recv_sem,
 ):
     a, b = lax.axis_index("wide"), lax.axis_index("narrow")
@@ -140,19 +140,21 @@
     def device(dx, dy):
         return (lax.rem(a + dx + n_wide, n_wide), lax.rem(b + dy + n_narrow, n_narrow))
 
-    pairs_of = [
+    small = [
         (cell_hbm, cell_ref), (off_hbm, off_ref), (slot_hbm, slot_ref), (src_hbm, src_ref), (tgt_hbm, tgt_ref),
-        (rad_hbm, rad_ref), (vel_hbm, vel_ref), (mig_hbm, mig_ref), (pdfs_hbm, pdfs),
-        (pairs_hbm, pairs_ref), (pos_hbm, pos_ref), (spring_hbm, spring_ref), (flags_hbm, flags),
+        (rad_hbm, rad_ref), (vel_hbm, vel_ref), (pairs_hbm, pairs_ref), (spring_hbm, spring_ref), (pos_hbm, pos_ref),
+        (mig_hbm, mig_ref),
     ]
-    loads = [pltpu.make_async_copy(x, y, load_sem.at[i]) for i, (x, y) in enumerate(pairs_of)]
+    parts = [slice(i * 256, (i + 1) * 256) for i in range(4)]
+    large = [(pdfs_hbm.at[:, :, part], pdfs.at[:, :, part]) for part in parts] + [(flags_hbm, flags)]
+    loads = [pltpu.make_async_copy(x, y, load_sem.at[i]) for i, (x, y) in enumerate(small + large)]
     for load in loads:
         load.start()
     around = [(dx, dy) for dx in (-1, 0, 1) for dy in (-1, 0, 1) if dx or dy] + [(-2, 0), (2, 0)]
     barrier = pltpu.get_barrier_semaphore()
     for dx, dy in around:
         pl.semaphore_signal(barrier, inc=1, device_id=device(dx, dy), device_id_type=MESH)
-    for load in loads[:8]:
+    for load in loads[:11]:
         load.wait()
 
     src_packed, tgt_packed, counts = pack_interface(off_ref, slot_ref, src_ref, tgt_ref)
@@ -221,92 +223,6 @@
             ext[q, out_rows, cols] = keep * p[q] + (even + odd)
             ext[q + 1, out_rows, cols] = keep * p[q + 1] + (even - odd)
 
-    bring(0)
-    loads[8].wait()
-    for i in range(2):
-        if i < 1:
-            bring(i + 1)
-        for col in range(i * 512, i * 512 + 512, 128):
-            for row in range(0, NX, 8):
-                collide(row, col)
-
-    for k in range(5):
-        edge_x[0, k:k + 1, :] = ext[X_PLUS[k], TOP + NX - 1:TOP + NX, :]
-        edge_x[1, k:k + 1, :] = ext[X_MINUS[k], TOP:TOP + 1, :]
-        edge_y[0, k] = ext[Y_PLUS[k], TOP:TOP + NX, 896:1024]
-        edge_y[1, k] = ext[Y_MINUS[k], TOP:TOP + NX, 0:128]
-    edge_c[0, 0:1, :] = ext[7, TOP + NX - 1:TOP + NX, 896:1024]
-    edge_c[1, 0:1, :] = ext[8, TOP:TOP + 1, 0:128]
-    edge_c[2, 0:1, :] = ext[9, TOP + NX - 1:TOP + NX, 0:128]
-    edge_c[3, 0:1, :] = ext[10, TOP:TOP + 1, 896:1024]
-    pl.semaphore_wait(barrier, len(around))
-
-    def send(index, source, target, dx, dy):
-        copy = pltpu.make_async_remote_copy(
-            src_ref=source, dst_ref=target, send_sem=send_sem.at[index], recv_sem=recv_sem.at[index],
-            device_id=device(dx, dy), device_id_type=MESH)
-        copy.start()
-        return copy
-
-    halo = [
-        send(0, edge_x.at[0], halo_x.at[0], 1, 0),
-        send(1, edge_x.at[1], halo_x.at[1], -1, 0),
-        send(2, edge_y.at[0], halo_y.at[0], 0, 1),
-        send(3, edge_y.at[1], halo_y.at[1], 0, -1),
-        send(4, edge_c.at[0], halo_c.at[0], 1, 1),
-        send(5, edge_c.at[1], halo_c.at[1], -1, -1),
-        send(6, edge_c.at[2], halo_c.at[2], 1, -1),
-        send(7, edge_c.at[3], halo_c.at[3], -1, 1),
-    ]
-
-    def fluid_at_grains():
-        for part, value in enumerate(split2(velf[...])):
-            velb[part * 96:part * 96 + 96, :] = value.astype(BF16)
-        for i in range(2):
-            cols = slice(i * 512, (i + 1) * 512)
-            got = dot(velb[...], onehot[:, cols], NN)
-            got = got[0:96] + got[96:192]
-            here = iota((NX, 512), 0) == (cell_ref[:, cols] >> 10)
-            for c in range(3):
-                fluid[c:c + 1, cols] = jnp.sum(jnp.where(here, got[c * NX:(c + 1) * NX], 0.0), axis=0, keepdims=True)
-
-    lane = iota((NX, 128), 1)
-
-    def stream(group):
-        for k, q in enumerate(group):
-            cx, cy, cz = VELOCITY[q]
-            shift = cy * 32 + cz
-            rows = slice(TOP - cx, TOP - cx + NX)
-            value = ext[q, rows, :]
-            if shift:
-                value = pltpu.roll(value, shift % NYZ, 1)
-            if cy == 1:
-                edge = pltpu.roll(halo_yp[0, Y_PLUS.index(q), rows, :], shift % 128, 1)
-                value = jnp.concatenate([jnp.where(lane < 32, edge, value[:, 0:128]), value[:, 128:]], axis=1)
-            if cy == -1:
-                edge = pltpu.roll(halo_yp[1, Y_MINUS.index(q), rows, :], shift % 128, 1)
-                value = jnp.concatenate([value[:, :896], jnp.where(lane >= 96, edge, value[:, 896:])], axis=1)
-            if q:
-                bit = 1 << (q if q < 10 else q - 10)
-                solid = (flags[0 if q < 10 else 1] & bit) != 0
-                value = jnp.where(solid, ext[OPPOSITE[q], TOP:TOP + NX, :], value)
-            read_ref[q] = value
-            high, low = split2(value)
-            at = group[0] * 2 * NX + k * NX
-            splits[at:at + NX, :] = high.astype(BF16)
-            splits[at + len(group) * NX:at + (len(group) + 1) * NX, :] = low.astype(BF16)
-
-    def extract(group, i, width=1):
-        cols = slice(i * 256, (i + width) * 256)
-        at, size = group[0] * 2 * NX, len(group) * NX
-        got = dot(splits[at:at + 2 * size, :], source_hot[:, cols], NN)
-        here = iota((NX, 256 * width), 0) == (src_packed[:, cols] >> 10)
-        for k, q in enumerate(group):
-            value = got[k * NX:(k + 1) * NX] + got[size + k * NX:size + (k + 1) * NX]
-            value = jnp.sum(jnp.where(here, value, 0.0), axis=0, keepdims=True)
-            for w in range(width):
-                gathered[i + w, q:q + 1, :] = value[:, w * 256:(w + 1) * 256]
-
     def contacts_in():
         vel8[...] = jnp.zeros_like(vel8)
         vel8[0:3, :] = vel_ref[...]
@@ -344,6 +260,93 @@
             summed[h * 16:h * 16 + 3] + summed[h * 16 + 3:h * 16 + 6] + summed[h * 16 + 6:h * 16 + 9] for h in range(8)]
         return jnp.concatenate(parts, axis=1)
 
+    bring(0)
+    contacts_in()
+    summed = contacts_out()
+    for i in range(4):
+        loads[11 + i].wait()
+    bring(1)
+    for col in range(0, NYZ, 128):
+        for row in range(0, NX, 8):
+            collide(row, col)
+
+    for k in range(5):
+        edge_x[0, k:k + 1, :] = ext[X_PLUS[k], TOP + NX - 1:TOP + NX, :]
+        edge_x[1, k:k + 1, :] = ext[X_MINUS[k], TOP:TOP + 1, :]
+        edge_y[0, k] = ext[Y_PLUS[k], TOP:TOP + NX, 896:1024]
+        edge_y[1, k] = ext[Y_MINUS[k], TOP:TOP + NX, 0:128]
+    edge_c[0, 0:1, :] = ext[7, TOP + NX - 1:TOP + NX, 896:1024]
+    edge_c[1, 0:1, :] = ext[8, TOP:TOP + 1, 0:128]
+    edge_c[2, 0:1, :] = ext[9, TOP + NX - 1:TOP + NX, 0:128]
+    edge_c[3, 0:1, :] = ext[10, TOP:TOP + 1, 896:1024]
+    pl.semaphore_wait(barrier, len(around))
+
+    def send(index, source, target, dx, dy):
+        copy = pltpu.make_async_remote_copy(
+            src_ref=source, dst_ref=target, send_sem=send_sem.at[index], recv_sem=recv_sem.at[index],
+            device_id=device(dx, dy), device_id_type=MESH)
+        copy.start()
+        return copy
+
+    halo = [
+        send(0, edge_x.at[0], halo_x.at[0], 1, 0),
+        send(1, edge_x.at[1], halo_x.at[1], -1, 0),
+        send(2, edge_y.at[0], halo_y.at[0], 0, 1),
+        send(3, edge_y.at[1], halo_y.at[1], 0, -1),
+        send(4, edge_c.at[0], halo_c.at[0], 1, 1),
+        send(5, edge_c.at[1], halo_c.at[1], -1, -1),
+        send(6, edge_c.at[2], halo_c.at[2], 1, -1),
+        send(7, edge_c.at[3], halo_c.at[3], -1, 1),
+    ]
+
+    def fluid_at_grains():
+        for part, value in enumerate(split2(velf[...])):
+            velb[part * 96:part * 96 + 96, :] = value.astype(BF16)
+        for i in range(2):
+            cols = slice(i * 512, (i + 1) * 512)
+            got = dot(velb[...], onehot[:, cols], NN)
+            got = got[0:96] + got[96:192]
+            here = iota((NX, 512), 0) == (cell_ref[:, cols] >> 10)
+            for c in range(3):
+                fluid[c:c + 1, cols] = jnp.sum(jnp.where(here, got[c * NX:(c + 1) * NX], 0.0), axis=0, keepdims=True)
+
+    lane = iota((NX, 128), 1)
+
+    def stream(group):
+        for k, q in enumerate(group):
+            cx, cy, cz = VELOCITY[q]
+            shift = cy * 32 + cz
+            rows = slice(TOP - cx, TOP - cx + NX)
+            value = ext[q, rows, :]
+            if shift:
+                value = pltpu.roll(value, shift % NYZ, 1)
+            if cy == 1:
+                edge = pltpu.roll(halo_yp[0, Y_PLUS.index(q), rows, :], shift % 128, 1)
+                value = jnp.concatenate([jnp.where(lane < 32, edge, value[:, 0:128]), value[:, 128:]], axis=1)
+            if cy == -1:
+                edge = pltpu.roll(halo_yp[1, Y_MINUS.index(q), rows, :], shift % 128, 1)
+                value = jnp.concatenate([value[:, :896], jnp.where(lane >= 96, edge, value[:, 896:])], axis=1)
+            if q:
+                bit = 1 << (q if q < 10 else q - 10)
+                solid = (flags[0 if q < 10 else 1] & bit) != 0
+                value = jnp.where(solid, ext[OPPOSITE[q], TOP:TOP + NX, :], value)
+            read_ref[q] = value
+            high = value.astype(BF16)
+            at = group[0] * 2 * NX + k * NX
+            splits[at:at + NX, :] = high
+            splits[at + len(group) * NX:at + (len(group) + 1) * NX, :] = (value - high.astype(F32)).astype(BF16)
+
+    def extract(group, i, width=1):
+        cols = slice(i * 256, (i + width) * 256)
+        at, size = group[0] * 2 * NX, len(group) * NX
+        got = dot(splits[at:at + 2 * size, :], source_hot[:, cols], NN)
+        here = iota((NX, 256 * width), 0) == (src_packed[:, cols] >> 10)
+        for k, q in enumerate(group):
+            value = got[k * NX:(k + 1) * NX] + got[size + k * NX:size + (k + 1) * NX]
+            value = jnp.sum(jnp.where(here, value, 0.0), axis=0, keepdims=True)
+            for w in range(width):
+                gathered[i + w, q:q + 1, :] = value[:, w * 256:(w + 1) * 256]
+
     def move_grains(summed):
         radius = rad_ref[...]
         vel = vel_ref[...]
@@ -367,8 +370,8 @@
     def send_region(i):
         rows_out.append(send(10 + i, gathered.at[i], received.at[i], DISTANCE[i], 0))
 
-    for load in loads[9:]:
-        load.wait()
+    fluid_at_grains()
+    loads[15].wait()
     for copy in halo:
         copy.wait()
     for k in range(5):
@@ -381,24 +384,15 @@
     halo_yp[1, 2, TOP - 1:TOP, :] = halo_c[2, 0:1, :]
     halo_yp[0, 2, TOP + NX:TOP + NX + 1, :] = halo_c[3, 0:1, :]
     stream(GROUPS[0])
-    fluid_at_grains()
     extract(GROUPS[0], 0, 2)
-    contacts_in()
-    summed = contacts_out()
     send_region(0)
     send_region(1)
     extract(GROUPS[0], 2, 2)
+    send_region(2)
+    send_region(3)
     move_grains(summed)
     leave()
     migrate = [send(8, leaving, joined.at[0], -1, 0), send(9, leaving, joined.at[1], 1, 0)]
-    send_region(2)
-    send_region(3)
-
-    for copy in migrate:
-        copy.wait()
-    mig_lane = iota((8, 128), 1)
-    change = jnp.where(iota((8, 128), 0) == 0, jnp.where(mig_lane < 64, float(NX), -float(NX)), 0.0)
-    newcomers_ref[...] = jnp.where(mig_lane < 64, joined[0], joined[1]) + change
 
     for i in range(4):
         cols = slice(i * 256, (i + 1) * 256)
@@ -411,31 +405,34 @@
                 spread_ref[(part * 19 + q) * NX:(part * 19 + q + 1) * NX, cols] = jnp.where(here, value, 0.0).astype(BF16)
         spread_ref[38 * NX:39 * NX, cols] = jnp.where(here, 1.0, 0.0).astype(BF16)
 
+    for copy in migrate:
+        copy.wait()
+    mig_lane = iota((8, 128), 1)
+    change = jnp.where(iota((8, 128), 0) == 0, jnp.where(mig_lane < 64, float(NX), -float(NX)), 0.0)
+    newcomers = jnp.where(mig_lane < 64, joined[0], joined[1]) + change
+    slots = jnp.concatenate([mig_ref[0:1, :], mig_ref[1:2, :]], axis=1)
+    placed = dot(jnp.concatenate(split3(newcomers), axis=0).astype(BF16), one_hot(slots, NYZ), NT)
+    placed = placed[0:8] + placed[8:16] + placed[16:24]
+    result_ref[...] = jnp.where(placed[7:8] > 0.5, placed, state_ref[...])
+
 
 def finish_kernel(
-    read_ref, spread_ref, tgtp_ref, state_ref, newcomers_ref, mig_ref, spring_ref,
+    read_ref, spread_ref, tgtp_ref, result_ref, spring_ref,
     next_hbm, pos_hbm, vel_hbm, rad_hbm, spring_hbm,
     blended, pos, vel, rad, sem,
 ):
-    copies = [pltpu.make_async_copy(spring_ref, spring_hbm, sem.at[0])]
-    copies[0].start()
-
-    slots = jnp.concatenate([mig_ref[0:1, :], mig_ref[1:2, :]], axis=1)
-    arrived = jnp.concatenate(split3(newcomers_ref[...]), axis=0).astype(BF16)
-    placed = dot(arrived, one_hot(slots, NYZ), NT)
-    placed = placed[0:8] + placed[8:16] + placed[16:24]
-    result = jnp.where(placed[7:8] > 0.5, placed, state_ref[...])
-    pos[...] = result[0:3]
-    vel[...] = result[3:6]
-    rad[...] = result[6:7]
-    for source, target in ((pos, pos_hbm), (vel, vel_hbm), (rad, rad_hbm)):
+    pos[...] = result_ref[0:3, :]
+    vel[...] = result_ref[3:6, :]
+    rad[...] = result_ref[6:7, :]
+    copies = []
+    for source, target in ((spring_ref, spring_hbm), (pos, pos_hbm), (vel, vel_hbm), (rad, rad_hbm)):
         copies.append(pltpu.make_async_copy(source, target, sem.at[len(copies)]))
         copies[-1].start()
 
     row = tgtp_ref[...] & 1023
-    for i in range(4):
-        cols = slice(i * 256, (i + 1) * 256)
-        got = dot(spread_ref[...], one_hot(row, 256, i * 256), NT)
+    for i in range(2):
+        cols = slice(i * 512, (i + 1) * 512)
+        got = dot(spread_ref[...], one_hot(row, 512, i * 512), NT)
         hit = got[38 * NX:39 * NX] > 0.5
         for start, stop in ((0, 10), (10, 19)):
             for q in range(start, stop):
@@ -464,11 +461,10 @@
             pltpu.VMEM((39 * NX, NYZ), BF16),
             pltpu.VMEM(row, jnp.int32),
             pltpu.VMEM((8, NYZ), F32),
-            pltpu.VMEM((8, 128), F32),
             pltpu.VMEM((3, 3072), F32),
         ),
         in_specs=[hbm] * 2 + [pl.BlockSpec(memory_space=pltpu.SMEM)] + [hbm] * 11,
-        out_specs=(vmem,) * 6,
+        out_specs=(vmem,) * 5,
         scratch_shapes=[
             pltpu.VMEM((19, NX, NYZ), F32),
             pltpu.VMEM((2, NX, NYZ), jnp.int32),
@@ -505,7 +501,8 @@
             pltpu.VMEM((2, 8, 128), F32),
             pltpu.VMEM((8, NYZ), F32),
             pltpu.VMEM((4 * NX, NYZ), F32),
-            pltpu.SemaphoreType.DMA((14,)),
+            pltpu.VMEM((8, NYZ), F32),
+            pltpu.SemaphoreType.DMA((16,)),
             pltpu.SemaphoreType.DMA((14,)),
             pltpu.SemaphoreType.DMA((14,)),
         ],
@@ -515,7 +512,7 @@
         contact_spring, iface_source.reshape(row), iface_offset.reshape(row), iface_slot.reshape(row),
         iface_target.reshape(8, 128), migrant_slots,
     )
-    read, spread, tgtp, state, newcomers, spring_next = outs
+    read, spread, tgtp, state, spring_next = outs
     result = pl.pallas_call(
         finish_kernel,
         name="finish",
@@ -526,7 +523,7 @@
             jax.ShapeDtypeStruct(row, F32),
             jax.ShapeDtypeStruct((3, 3072), F32),
         ),
-        in_specs=[vmem] * 7,
+        in_specs=[vmem] * 5,
         out_specs=(hbm,) * 5,
         scratch_shapes=[
             pltpu.VMEM((19, NX, NYZ), F32),
@@ -536,7 +533,7 @@
             pltpu.SemaphoreType.DMA((12,)),
         ],
         compiler_params=pltpu.CompilerParams(vmem_limit_bytes=40 << 20),
-    )(read, spread, tgtp, state, newcomers, migrant_slots, spring_next)
+    )(read, spread, tgtp, state, spring_next)
     pdfs_next, pos_next, vel_next, rad_next, spring_out = result
     return pdfs_next, pos_next, vel_next, rad_next.reshape(NYZ), spring_out
 

time: 30 us -> 29.6 us (0.987)
  Pallas kernels: 28.5 us -> 28.2 us
where the time goes in v3:
time: 29.6 us; the launch traced here: 29.4 us
  Pallas kernels  28.2 us (95%)
  between operations  1.29 us (4%)
    pallas_call x1, Pallas kernels, shards(): pl.pallas_call(step_kernel, name='step', out_shape=(pltpu.VMEM((19, NX, N...  23.7 us
    pallas_call x1, Pallas kernels, shards(): pl.pallas_call(finish_kernel, name='finish', out_shape=(jax.ShapeDtypeStr...  4.44 us

profile of v3, /device:TPU:1, one launch (start us, length us, event | category | flops | bytes accessed | tf_op | source)
XLA Modules:
  0.0 29.4 jit_solution(13596037749271317328)
XLA Ops:
  1.3 23.7 %step.1 = (f32[19,32,1024]{2,1,0:T(8,128)S(1)}, bf16[1248,1024]{1,0:T(8,128)(2,1)S(1)}, s32[1,1024]{1,0:T(1,128)S(1)}, f32[8,1024]{1,0:T(8,128)S(1)}, f32[3,3072]{1,0:T(4,128)S(1)}) custom-call(f32[19,32,1024]{2,1,0:T(8,128)} %pdfs_hbm.1, s32[2,32,1024]{2,1,0:T(8,128)} %flags_hbm.1, s32[1,1]{1,0:T(1,128)S(6)} %copy.19.level_ref, f32[3,1024]{1,0:T(4,128)} %pos_hbm.1, ...), custom_call_target="tpu_custom_call" | custom-call | tf_op jit(solution)/shard_map/step/pallas_call | solution.py:456
  25.0 4.4 %finish.1 = (f32[19,32,1024]{2,1,0:T(8,128)}, f32[3,1024]{1,0:T(4,128)}, f32[3,1024]{1,0:T(4,128)}, f32[1,1024]{1,0:T(1,128)}, f32[3,3072]{1,0:T(4,128)}) custom-call(f32[19,32,1024]{2,1,0:T(8,128)S(1)} %get-tuple-element.15.read_ref, bf16[1248,1024]{1,0:T(8,128)(2,1)S(1)} %get-tuple-element.16.spread_ref, s32[1,1024]{1,0:T(1,128)S(1)} %get-tuple-element.17.tgtp_ref, ...), custom_call_target="tpu_custom_call" | custom-call | tf_op jit(solution)/shard_map/finish/pallas_call | solution.py:516

commit v4 on v3

--- a/solution.py
+++ b/solution.py
@@ -63,8 +63,10 @@
 
 
 def fill_one_hot(ref, row):
-    for start in range(0, NYZ, 128):
-        ref[start:start + 128, :] = one_hot(row, 128, start)
+    low = one_hot(row & 31, 32)
+    high = one_hot(row >> 5, 32)
+    for y in range(32):
+        ref[y * 32:y * 32 + 32, :] = low * high[y:y + 1, :]
 
 
 def dot(a, b, dims):
@@ -125,10 +127,10 @@
 
 
 def step_kernel(
-    pdfs_hbm, flags_hbm, level_ref, pos_hbm, vel_hbm, rad_hbm, cell_hbm, pairs_hbm, spring_hbm, src_hbm, off_hbm, slot_hbm,
+    pdfs_hbm, flags_hbm, level_hbm, pos_hbm, vel_hbm, rad_hbm, cell_hbm, pairs_hbm, spring_hbm, src_hbm, off_hbm, slot_hbm,
     tgt_hbm, mig_hbm,
     read_ref, spread_ref, tgtp_ref, result_ref, spring_out_ref,
-    pdfs, flags, pos_ref, vel_ref, rad_ref, cell_ref, pairs_ref, spring_ref, src_ref, off_ref, slot_ref, tgt_ref,
+    pdfs, flags, level, pos_ref, vel_ref, rad_ref, cell_ref, pairs_ref, spring_ref, src_ref, off_ref, slot_ref, tgt_ref,
     mig_ref,
     onehot, source_hot, moved_in, ext, velf, velb, vel8, rows16, edge_x, edge_y, edge_c, halo_x, halo_y, halo_yp, halo_c, splits,
     gathered, received, leaving, joined, fluid, force, state_ref,
@@ -143,7 +145,7 @@
     small = [
         (cell_hbm, cell_ref), (off_hbm, off_ref), (slot_hbm, slot_ref), (src_hbm, src_ref), (tgt_hbm, tgt_ref),
         (rad_hbm, rad_ref), (vel_hbm, vel_ref), (pairs_hbm, pairs_ref), (spring_hbm, spring_ref), (pos_hbm, pos_ref),
-        (mig_hbm, mig_ref),
+        (mig_hbm, mig_ref), (level_hbm, level),
     ]
     parts = [slice(i * 256, (i + 1) * 256) for i in range(4)]
     large = [(pdfs_hbm.at[:, :, part], pdfs.at[:, :, part]) for part in parts] + [(flags_hbm, flags)]
@@ -154,7 +156,7 @@
     barrier = pltpu.get_barrier_semaphore()
     for dx, dy in around:
         pl.semaphore_signal(barrier, inc=1, device_id=device(dx, dy), device_id_type=MESH)
-    for load in loads[:11]:
+    for load in loads[:12]:
         load.wait()
 
     src_packed, tgt_packed, counts = pack_interface(off_ref, slot_ref, src_ref, tgt_ref)
@@ -164,14 +166,14 @@
     grain_x = cell >> 10
     fill_one_hot(onehot, cell & 1023)
     drag = drag_coef * rad_ref[...]
-    in_row = iota((NX, NYZ), 0) == grain_x
+    in_row = one_hot(grain_x, NX)
     weights = [drag] + [drag * vel_ref[c:c + 1, :] for c in range(3)]
     for k, weight in enumerate(weights):
         for part, value in enumerate(split2(weight)):
-            moved_in[(part * 4 + k) * NX:(part * 4 + k + 1) * NX, :] = jnp.where(in_row, value, 0.0).astype(BF16)
+            moved_in[(part * 4 + k) * NX:(part * 4 + k + 1) * NX, :] = in_row * value.astype(BF16)
     fill_one_hot(source_hot, src_packed & 1023)
 
-    fine = level_ref[0, 0] == 1
+    fine = level[0] == 1
     tau = jnp.where(fine, tau_fine, tau_coarse).astype(F32)
     omega = jnp.where(fine, 1.0 / tau_fine, 1.0 / tau_coarse).astype(F32)
     keep = jnp.where(fine, 1.0 - 1.0 / tau_fine, 0.0).astype(F32)
@@ -264,7 +266,7 @@
     contacts_in()
     summed = contacts_out()
     for i in range(4):
-        loads[11 + i].wait()
+        loads[12 + i].wait()
     bring(1)
     for col in range(0, NYZ, 128):
         for row in range(0, NX, 8):
@@ -273,8 +275,12 @@
     for k in range(5):
         edge_x[0, k:k + 1, :] = ext[X_PLUS[k], TOP + NX - 1:TOP + NX, :]
         edge_x[1, k:k + 1, :] = ext[X_MINUS[k], TOP:TOP + 1, :]
-        edge_y[0, k] = ext[Y_PLUS[k], TOP:TOP + NX, 896:1024]
-        edge_y[1, k] = ext[Y_MINUS[k], TOP:TOP + NX, 0:128]
+    group = iota((NX, 128), 1) >> 5
+    for side, (dirs, start, base) in enumerate(((Y_PLUS, 896, 32), (Y_MINUS, 0, 0))):
+        tiles = [ext[q, TOP:TOP + NX, start:start + 128] for q in dirs]
+        moved = [pltpu.roll(t, (base + 32 * k) % 128, 1) if (base + 32 * k) % 128 else t for k, t in enumerate(tiles)]
+        edge_y[side, 0] = jnp.where(group == 0, moved[0], jnp.where(group == 1, moved[1], jnp.where(group == 2, moved[2], moved[3])))
+        edge_y[side, 1] = moved[4]
     edge_c[0, 0:1, :] = ext[7, TOP + NX - 1:TOP + NX, 896:1024]
     edge_c[1, 0:1, :] = ext[8, TOP:TOP + 1, 0:128]
     edge_c[2, 0:1, :] = ext[9, TOP + NX - 1:TOP + NX, 0:128]
@@ -289,14 +295,14 @@
         return copy
 
     halo = [
+        send(4, edge_c.at[0], halo_c.at[0], 1, 1),
+        send(5, edge_c.at[1], halo_c.at[1], -1, -1),
+        send(6, edge_c.at[2], halo_c.at[2], 1, -1),
+        send(7, edge_c.at[3], halo_c.at[3], -1, 1),
         send(0, edge_x.at[0], halo_x.at[0], 1, 0),
         send(1, edge_x.at[1], halo_x.at[1], -1, 0),
         send(2, edge_y.at[0], halo_y.at[0], 0, 1),
         send(3, edge_y.at[1], halo_y.at[1], 0, -1),
-        send(4, edge_c.at[0], halo_c.at[0], 1, 1),
-        send(5, edge_c.at[1], halo_c.at[1], -1, -1),
-        send(6, edge_c.at[2], halo_c.at[2], 1, -1),
-        send(7, edge_c.at[3], halo_c.at[3], -1, 1),
     ]
 
     def fluid_at_grains():
@@ -371,14 +377,16 @@
         rows_out.append(send(10 + i, gathered.at[i], received.at[i], DISTANCE[i], 0))
 
     fluid_at_grains()
-    loads[15].wait()
+    loads[16].wait()
     for copy in halo:
         copy.wait()
     for k in range(5):
         ext[X_PLUS[k], TOP - 1:TOP, :] = halo_x[0, k:k + 1, :]
         ext[X_MINUS[k], TOP + NX:TOP + NX + 1, :] = halo_x[1, k:k + 1, :]
-        for side in range(2):
-            halo_yp[side, k, TOP:TOP + NX, :] = halo_y[side, k]
+        for side, base in enumerate((96, 0)):
+            back = (base - 32 * k) % 128
+            tile = halo_y[side, k // 4]
+            halo_yp[side, k, TOP:TOP + NX, :] = pltpu.roll(tile, back, 1) if back else tile
     halo_yp[0, 1, TOP - 1:TOP, :] = halo_c[0, 0:1, :]
     halo_yp[1, 1, TOP + NX:TOP + NX + 1, :] = halo_c[1, 0:1, :]
     halo_yp[1, 2, TOP - 1:TOP, :] = halo_c[2, 0:1, :]
@@ -399,11 +407,11 @@
         rows_out[i].wait()
         stays = iota((24, 256), 1).astype(F32) >= counts[i]
         carried = jnp.where(stays, gathered[i], received[i])
-        here = iota((NX, 256), 0) == (tgt_packed[:, cols] >> 10)
+        here = one_hot(tgt_packed[:, cols] >> 10, NX)
         for q in range(19):
             for part, value in enumerate(split2(carried[q:q + 1, :])):
-                spread_ref[(part * 19 + q) * NX:(part * 19 + q + 1) * NX, cols] = jnp.where(here, value, 0.0).astype(BF16)
-        spread_ref[38 * NX:39 * NX, cols] = jnp.where(here, 1.0, 0.0).astype(BF16)
+                spread_ref[(part * 19 + q) * NX:(part * 19 + q + 1) * NX, cols] = here * value.astype(BF16)
+        spread_ref[38 * NX:39 * NX, cols] = here
 
     for copy in migrate:
         copy.wait()
@@ -463,11 +471,12 @@
             pltpu.VMEM((8, NYZ), F32),
             pltpu.VMEM((3, 3072), F32),
         ),
-        in_specs=[hbm] * 2 + [pl.BlockSpec(memory_space=pltpu.SMEM)] + [hbm] * 11,
+        in_specs=[hbm] * 14,
         out_specs=(vmem,) * 5,
         scratch_shapes=[
             pltpu.VMEM((19, NX, NYZ), F32),
             pltpu.VMEM((2, NX, NYZ), jnp.int32),
+            pltpu.SMEM((1,), jnp.int32),
             pltpu.VMEM((3, NYZ), F32),
             pltpu.VMEM((3, NYZ), F32),
             pltpu.VMEM(row, F32),
@@ -488,10 +497,10 @@
             pltpu.VMEM((8, NYZ), F32),
             pltpu.VMEM((16, 3072), F32),
             pltpu.VMEM((2, 8, NYZ), F32),
-            pltpu.VMEM((2, 5, NX, 128), F32),
+            pltpu.VMEM((2, 2, NX, 128), F32),
             pltpu.VMEM((4, 8, 128), F32),
             pltpu.VMEM((2, 8, NYZ), F32),
-            pltpu.VMEM((2, 5, NX, 128), F32),
+            pltpu.VMEM((2, 2, NX, 128), F32),
             pltpu.VMEM((2, 5, EXT, 128), F32),
             pltpu.VMEM((4, 8, 128), F32),
             pltpu.VMEM((38 * NX, NYZ), BF16),
@@ -502,13 +511,13 @@
             pltpu.VMEM((8, NYZ), F32),
             pltpu.VMEM((4 * NX, NYZ), F32),
             pltpu.VMEM((8, NYZ), F32),
-            pltpu.SemaphoreType.DMA((16,)),
+            pltpu.SemaphoreType.DMA((17,)),
             pltpu.SemaphoreType.DMA((14,)),
             pltpu.SemaphoreType.DMA((14,)),
         ],
         compiler_params=pltpu.CompilerParams(collective_id=0, has_side_effects=True, vmem_limit_bytes=61_800_000),
     )(
-        pdfs, link_flags, block_level, grain_pos, grain_vel, grain_radius.reshape(row), grain_cell.reshape(row), contact_pairs,
+        pdfs, link_flags, block_level.reshape(1), grain_pos, grain_vel, grain_radius.reshape(row), grain_cell.reshape(row), contact_pairs,
         contact_spring, iface_source.reshape(row), iface_offset.reshape(row), iface_slot.reshape(row),
         iface_target.reshape(8, 128), migrant_slots,
     )

time: 29.6 us -> 29.3 us (0.990)
  Pallas kernels: 28.2 us -> 27.9 us
where the time goes in v4:
time: 29.3 us; the launch traced here: 29.2 us
  Pallas kernels  27.9 us (95%)
  between operations  1.29 us (4%)
    pallas_call x1, Pallas kernels, shards(): pl.pallas_call(step_kernel, name='step', out_shape=(pltpu.VMEM((19, NX, N...  23.5 us
    pallas_call x1, Pallas kernels, shards(): pl.pallas_call(finish_kernel, name='finish', out_shape=(jax.ShapeDtypeStr...  4.44 us

profile of v4, /device:TPU:1, one launch (start us, length us, event | category | flops | bytes accessed | tf_op | source)
XLA Modules:
  0.0 29.2 jit_solution(6627871409584383305)
XLA Ops:
  1.3 23.5 %step.1 = (f32[19,32,1024]{2,1,0:T(8,128)S(1)}, bf16[1248,1024]{1,0:T(8,128)(2,1)S(1)}, s32[1,1024]{1,0:T(1,128)S(1)}, f32[8,1024]{1,0:T(8,128)S(1)}, f32[3,3072]{1,0:T(4,128)S(1)}) custom-call(f32[19,32,1024]{2,1,0:T(8,128)} %pdfs_hbm.1, s32[2,32,1024]{2,1,0:T(8,128)} %flags_hbm.1, s32[1]{0:T(128)} %bitcast.8.level_hbm, f32[3,1024]{1,0:T(4,128)} %pos_hbm.1, ...), custom_call_target="tpu_custom_call" | custom-call | tf_op jit(solution)/shard_map/step/pallas_call | solution.py:464
  24.7 4.4 %finish.1 = (f32[19,32,1024]{2,1,0:T(8,128)}, f32[3,1024]{1,0:T(4,128)}, f32[3,1024]{1,0:T(4,128)}, f32[1,1024]{1,0:T(1,128)}, f32[3,3072]{1,0:T(4,128)}) custom-call(f32[19,32,1024]{2,1,0:T(8,128)S(1)} %get-tuple-element.15.read_ref, bf16[1248,1024]{1,0:T(8,128)(2,1)S(1)} %get-tuple-element.16.spread_ref, s32[1,1024]{1,0:T(1,128)S(1)} %get-tuple-element.17.tgtp_ref, ...), custom_call_target="tpu_custom_call" | custom-call | tf_op jit(solution)/shard_map/finish/pallas_call | solution.py:525

commit v5 on v4

--- a/solution.py
+++ b/solution.py
@@ -133,7 +133,7 @@
     pdfs, flags, level, pos_ref, vel_ref, rad_ref, cell_ref, pairs_ref, spring_ref, src_ref, off_ref, slot_ref, tgt_ref,
     mig_ref,
     onehot, source_hot, moved_in, ext, velf, velb, vel8, rows16, edge_x, edge_y, edge_c, halo_x, halo_y, halo_yp, halo_c, splits,
-    gathered, received, leaving, joined, fluid, force, state_ref,
+    gathered, received, leaving, joined, fluid, force, state_ref, pull_ref,
     load_sem, send_sem, recv_sem,
 ):
     a, b = lax.axis_index("wide"), lax.axis_index("narrow")
@@ -263,8 +263,6 @@
         return jnp.concatenate(parts, axis=1)
 
     bring(0)
-    contacts_in()
-    summed = contacts_out()
     for i in range(4):
         loads[12 + i].wait()
     bring(1)
@@ -376,6 +374,8 @@
     def send_region(i):
         rows_out.append(send(10 + i, gathered.at[i], received.at[i], DISTANCE[i], 0))
 
+    contacts_in()
+    pull_ref[...] = contacts_out()
     fluid_at_grains()
     loads[16].wait()
     for copy in halo:
@@ -398,7 +398,7 @@
     extract(GROUPS[0], 2, 2)
     send_region(2)
     send_region(3)
-    move_grains(summed)
+    move_grains(pull_ref[...])
     leave()
     migrate = [send(8, leaving, joined.at[0], -1, 0), send(9, leaving, joined.at[1], 1, 0)]
 
@@ -511,6 +511,7 @@
             pltpu.VMEM((8, NYZ), F32),
             pltpu.VMEM((4 * NX, NYZ), F32),
             pltpu.VMEM((8, NYZ), F32),
+            pltpu.VMEM((3, NYZ), F32),
             pltpu.SemaphoreType.DMA((17,)),
             pltpu.SemaphoreType.DMA((14,)),
             pltpu.SemaphoreType.DMA((14,)),

time: 29.3 us -> 28.7 us (0.980)
  Pallas kernels: 27.9 us -> 27.3 us
    pallas_call x1, Pallas kernels: 23.5 us -> 22.9 us  [shards(): pl.pallas_call(step_kernel, name='step', out_shape=(pltpu.VMEM((19, NX, N...]
where the time goes in v5:
time: 28.7 us; the launch traced here: 28.6 us
  Pallas kernels  27.3 us (95%)
  between operations  1.29 us (4%)
    pallas_call x1, Pallas kernels, shards(): pl.pallas_call(step_kernel, name='step', out_shape=(pltpu.VMEM((19, NX, N...  22.9 us
    pallas_call x1, Pallas kernels, shards(): pl.pallas_call(finish_kernel, name='finish', out_shape=(jax.ShapeDtypeStr...  4.45 us

profile of v5, /device:TPU:1, one launch (start us, length us, event | category | flops | bytes accessed | tf_op | source)
XLA Modules:
  0.0 28.6 jit_solution(4687241444996880015)
XLA Ops:
  1.3 22.9 %step.1 = (f32[19,32,1024]{2,1,0:T(8,128)S(1)}, bf16[1248,1024]{1,0:T(8,128)(2,1)S(1)}, s32[1,1024]{1,0:T(1,128)S(1)}, f32[8,1024]{1,0:T(8,128)S(1)}, f32[3,3072]{1,0:T(4,128)S(1)}) custom-call(f32[19,32,1024]{2,1,0:T(8,128)} %pdfs_hbm.1, s32[2,32,1024]{2,1,0:T(8,128)} %flags_hbm.1, s32[1]{0:T(128)} %bitcast.8.level_hbm, f32[3,1024]{1,0:T(4,128)} %pos_hbm.1, ...), custom_call_target="tpu_custom_call" | custom-call | tf_op jit(solution)/shard_map/step/pallas_call | solution.py:464
  24.2 4.4 %finish.1 = (f32[19,32,1024]{2,1,0:T(8,128)}, f32[3,1024]{1,0:T(4,128)}, f32[3,1024]{1,0:T(4,128)}, f32[1,1024]{1,0:T(1,128)}, f32[3,3072]{1,0:T(4,128)}) custom-call(f32[19,32,1024]{2,1,0:T(8,128)S(1)} %get-tuple-element.15.read_ref, bf16[1248,1024]{1,0:T(8,128)(2,1)S(1)} %get-tuple-element.16.spread_ref, s32[1,1024]{1,0:T(1,128)S(1)} %get-tuple-element.17.tgtp_ref, ...), custom_call_target="tpu_custom_call" | custom-call | tf_op jit(solution)/shard_map/finish/pallas_call | solution.py:526

commit v6 on v5

--- a/solution.py
+++ b/solution.py
@@ -263,12 +263,14 @@
         return jnp.concatenate(parts, axis=1)
 
     bring(0)
-    for i in range(4):
-        loads[12 + i].wait()
-    bring(1)
-    for col in range(0, NYZ, 128):
-        for row in range(0, NX, 8):
-            collide(row, col)
+    for half in range(2):
+        loads[12 + 2 * half].wait()
+        loads[13 + 2 * half].wait()
+        if half == 0:
+            bring(1)
+        for col in range(half * 512, half * 512 + 512, 128):
+            for row in range(0, NX, 8):
+                collide(row, col)
 
     for k in range(5):
         edge_x[0, k:k + 1, :] = ext[X_PLUS[k], TOP + NX - 1:TOP + NX, :]
@@ -395,7 +397,11 @@
     extract(GROUPS[0], 0, 2)
     send_region(0)
     send_region(1)
-    extract(GROUPS[0], 2, 2)
+
+    @pl.when(a >= 0)
+    def _():
+        extract(GROUPS[0], 2, 2)
+
     send_region(2)
     send_region(3)
     move_grains(pull_ref[...])

time: 28.7 us -> 29 us (1.010)
  Pallas kernels: 27.3 us -> 27.6 us
    pallas_call x1, Pallas kernels: 22.9 us -> 23.2 us  [shards(): pl.pallas_call(step_kernel, name='step', out_shape=(pltpu.VMEM((19, NX, N...]
where the time goes in v6:
time: 29 us; the launch traced here: 28.9 us
  Pallas kernels  27.6 us (95%)
  between operations  1.29 us (4%)
    pallas_call x1, Pallas kernels, shards(): pl.pallas_call(step_kernel, name='step', out_shape=(pltpu.VMEM((19, NX, N...  23.2 us
    pallas_call x1, Pallas kernels, shards(): pl.pallas_call(finish_kernel, name='finish', out_shape=(jax.ShapeDtypeStr...  4.45 us

profile of v6, /device:TPU:1, one launch (start us, length us, event | category | flops | bytes accessed | tf_op | source)
XLA Modules:
  0.0 28.9 jit_solution(8102179203755416721)
XLA Ops:
  1.3 23.2 %step.1 = (f32[19,32,1024]{2,1,0:T(8,128)S(1)}, bf16[1248,1024]{1,0:T(8,128)(2,1)S(1)}, s32[1,1024]{1,0:T(1,128)S(1)}, f32[8,1024]{1,0:T(8,128)S(1)}, f32[3,3072]{1,0:T(4,128)S(1)}) custom-call(f32[19,32,1024]{2,1,0:T(8,128)} %pdfs_hbm.1, s32[2,32,1024]{2,1,0:T(8,128)} %flags_hbm.1, s32[1]{0:T(128)} %bitcast.8.level_hbm, f32[3,1024]{1,0:T(4,128)} %pos_hbm.1, ...), custom_call_target="tpu_custom_call" | custom-call | tf_op jit(solution)/shard_map/step/pallas_call | solution.py:470
  24.5 4.4 %finish.1 = (f32[19,32,1024]{2,1,0:T(8,128)}, f32[3,1024]{1,0:T(4,128)}, f32[3,1024]{1,0:T(4,128)}, f32[1,1024]{1,0:T(1,128)}, f32[3,3072]{1,0:T(4,128)}) custom-call(f32[19,32,1024]{2,1,0:T(8,128)S(1)} %get-tuple-element.15.read_ref, bf16[1248,1024]{1,0:T(8,128)(2,1)S(1)} %get-tuple-element.16.spread_ref, s32[1,1024]{1,0:T(1,128)S(1)} %get-tuple-element.17.tgtp_ref, ...), custom_call_target="tpu_custom_call" | custom-call | tf_op jit(solution)/shard_map/finish/pallas_call | solution.py:532

commit v7 on v6

--- a/solution.py
+++ b/solution.py
@@ -397,11 +397,7 @@
     extract(GROUPS[0], 0, 2)
     send_region(0)
     send_region(1)
-
-    @pl.when(a >= 0)
-    def _():
-        extract(GROUPS[0], 2, 2)
-
+    extract(GROUPS[0], 2, 2)
     send_region(2)
     send_region(3)
     move_grains(pull_ref[...])

time: 29 us -> 28.8 us (level)
  no operation moved by 1% of the time
where the time goes in v7:
time: 28.8 us; the launch traced here: 28.7 us
  Pallas kernels  27.4 us (95%)
  between operations  1.29 us (4%)
    pallas_call x1, Pallas kernels, shards(): pl.pallas_call(step_kernel, name='step', out_shape=(pltpu.VMEM((19, NX, N...  22.9 us
    pallas_call x1, Pallas kernels, shards(): pl.pallas_call(finish_kernel, name='finish', out_shape=(jax.ShapeDtypeStr...  4.44 us

profile of v7, /device:TPU:1, one launch (start us, length us, event | category | flops | bytes accessed | tf_op | source)
XLA Modules:
  0.0 28.7 jit_solution(18303644023809591975)
XLA Ops:
  1.3 22.9 %step.1 = (f32[19,32,1024]{2,1,0:T(8,128)S(1)}, bf16[1248,1024]{1,0:T(8,128)(2,1)S(1)}, s32[1,1024]{1,0:T(1,128)S(1)}, f32[8,1024]{1,0:T(8,128)S(1)}, f32[3,3072]{1,0:T(4,128)S(1)}) custom-call(f32[19,32,1024]{2,1,0:T(8,128)} %pdfs_hbm.1, s32[2,32,1024]{2,1,0:T(8,128)} %flags_hbm.1, s32[1]{0:T(128)} %bitcast.8.level_hbm, f32[3,1024]{1,0:T(4,128)} %pos_hbm.1, ...), custom_call_target="tpu_custom_call" | custom-call | tf_op jit(solution)/shard_map/step/pallas_call | solution.py:466
  24.2 4.4 %finish.1 = (f32[19,32,1024]{2,1,0:T(8,128)}, f32[3,1024]{1,0:T(4,128)}, f32[3,1024]{1,0:T(4,128)}, f32[1,1024]{1,0:T(1,128)}, f32[3,3072]{1,0:T(4,128)}) custom-call(f32[19,32,1024]{2,1,0:T(8,128)S(1)} %get-tuple-element.15.read_ref, bf16[1248,1024]{1,0:T(8,128)(2,1)S(1)} %get-tuple-element.16.spread_ref, s32[1,1024]{1,0:T(1,128)S(1)} %get-tuple-element.17.tgtp_ref, ...), custom_call_target="tpu_custom_call" | custom-call | tf_op jit(solution)/shard_map/finish/pallas_call | solution.py:528
